TPU v7x, 256 devices: a whole 4x4x8 slice. The times are simulated.
256 devices in a mesh: front: 8 (over x, core), grp: 32 (over y, z).
Axes of the slice: x: 4, y: 4, z: 8, core: 2. Of those that a mesh axis runs over, the one named last changes fastest.
Arguments:
- panel_block: bfloat16 [8, 4608, 1024], P('front', 'grp'), may hold values from -0.1796875 to 0.1796875
- trailing: float32 [8, 4608, 4608], P('front', 'grp')
- inverse: float32 [8, 1024, 1024], P('front')
- weights: float32 [8, 4608], P('front'), may hold values from -0.09375 to 0.09375
- live_size: int32 [8], P('front'), may hold values from 2304 to 4608, as said below
- column_source: int32 [8, 4608], P('front'), may hold values from 0 to 4607, each once within a row
- destination: int32 [8, 4608, 1], P('front', 'grp'), may hold values from 0 to 7; in each aligned block of 144 rows (0 to 143, 144 to 287, ..., all dimensions but the last counted through in order) at most 36 rows name the same one
- row_offset: int32 [8, 4608], P('front', 'grp'), may hold values from 0 to 143
Outputs:
- factor: float32 [8, 4608, 1024], P('front', 'grp')
- checksum: float32 [8, 4608], P('front', 'grp')
- ancestor: float32 [8, 4608, 4608], P('front', 'grp')
Inputs may be any that keep to these rules, and one draw needn't show every extreme that they name: `live_size`: each front's live size is 4608 minus a multiple of 576; one front is full. `destination`: among the 144 rows of one device at most 36 rows name the same ancestor front. `column_source`: each front's row is a permutation.
All inputs are finite; a program needn't handle non-finite values.
Results may differ from a plain program's by a relative error of at most 0.0003.
Values may be sent and summed in bfloat16 or wider, within the bound.
A program may use at most 128 MiB of HBM per device.

v0:
```python
import jax
import jax.numpy as jnp
from jax import lax
from jax.sharding import PartitionSpec as P


def place_columns(rows, source, live_count):
    keep_cols = (source < live_count).astype(jnp.float32)
    return jnp.take(rows, source, axis=1) * keep_cols[None, :]


def on_device(
    panel_block, trailing, inverse, weights, live_size, column_source, destination, row_offset
):
    highest_precision = lax.Precision.HIGHEST
    row_count = trailing.shape[1]
    col_count = trailing.shape[2]
    fronts = lax.axis_size("front")
    capacity = max(2, 2 * row_count // fronts)
    trail_rows = trailing[0]
    inverse_rows = inverse[0]
    live_count = live_size[0]
    panel_f32 = panel_block[0].astype(jnp.float32)
    factor = jnp.dot(panel_f32, inverse_rows.T, precision=highest_precision)
    update = lax.dot_general(
        factor,
        lax.all_gather(factor, "grp", axis=0, tiled=True),
        (((1,), (1,)), ((), ())),
        precision=highest_precision,
        preferred_element_type=jnp.float32,
    )
    schur_rows = trail_rows - update
    positions = jnp.arange(col_count, dtype=jnp.int32)
    colmask = (positions < live_count).astype(jnp.float32)
    masked_weights = weights[0] * colmask
    checksum = jnp.dot(schur_rows, masked_weights, precision=highest_precision)
    global_rows = lax.axis_index("grp") * row_count + jnp.arange(row_count, dtype=jnp.int32)
    live_rows = global_rows < live_count
    dest_front = destination[0, :, 0]
    front_ids = jnp.arange(fronts, dtype=jnp.int32)
    onehot = ((dest_front[:, None] == front_ids[None, :]) & live_rows[:, None]).astype(jnp.int32)
    running = jnp.cumsum(onehot, axis=0)
    slot_index = jnp.sum(onehot * (running - 1), axis=1)
    dest_live = jnp.where(live_rows, dest_front, fronts)
    row_tags = (
        jnp.full((fronts, capacity), -1.0, jnp.float32)
        .at[dest_live, slot_index]
        .set(row_offset[0].astype(jnp.float32), mode="drop")
    )
    permuted = place_columns(schur_rows, column_source[0], live_count)
    bucket = (
        jnp.zeros((fronts, capacity, col_count), jnp.float32)
        .at[dest_live, slot_index]
        .set(permuted, mode="drop")
    )
    received, received_tags = (
        lax.all_to_all(bucket, "front", split_axis=0, concat_axis=0, tiled=True),
        lax.all_to_all(row_tags, "front", split_axis=0, concat_axis=0, tiled=True),
    )
    flat_rows = received.reshape(fronts * capacity, col_count)
    flat_tags = received_tags.reshape(fronts * capacity)
    target_row = jnp.where(flat_tags < 0.0, row_count, flat_tags.astype(jnp.int32))
    ancestor = (
        jnp.zeros((row_count, col_count), jnp.float32).at[target_row].add(flat_rows, mode="drop")
    )
    return (factor[None], checksum[None], ancestor[None])


def solution(mesh):
    placed = (
        P("front", "grp", None),
        P("front", "grp", None),
        P("front", None, None),
        P("front", None),
        P("front"),
        P("front", None),
        P("front", "grp", None),
        P("front", "grp"),
    )
    return jax.shard_map(
        on_device,
        mesh=mesh,
        in_specs=placed,
        out_specs=(P("front", "grp", None), P("front", "grp"), P("front", "grp", None)),
        check_vma=False,
    )
```

profile of v0, /device:TPU:1, one launch (start us, length us, event | category | flops | bytes accessed | tf_op | source)
XLA Modules:
  0.0 367.1 jit_solution(13603879904250098993)
XLA Ops:
  7.2 0.0 copy-start
  7.2 0.0 copy-start.4
  7.2 0.0 copy-start.5
  7.2 0.0 copy-start.2
  7.2 0.0 all-gather.2.cloned.1.call-start
  7.3 0.9 copy-done
  8.1 5.4 %fusion = f32[144,1024]{1,0:T(8,128)} fusion(f32[1,1024,1024]{2,1,0:T(8,128)} %param.10, bf16[1,144,1024]{2,1,0:T(8,128)(2,1)S(1)} %copy-done), kind=kOutput, calls=%fused_computation.6 | convolution fusion | flops 1811939328 | bytes 5079040 | tf_op jit(solution)/shard_map/dot_general | solution.py:24
  13.6 0.0 all-gather.2.cloned.1.call-update
  14.3 0.0 copy-done.4
  14.3 0.6 reduce-window.6
  14.9 0.2 slice_reduce_fusion
  15.1 0.0 copy-done.5
  15.1 0.1 add_bitcast_fusion
  15.3 0.6 broadcast_in_dim.49
  15.9 22.1 %scatter_fusion = f32[8,36]{1,0:T(8,128)} fusion(f32[8,36]{1,0:T(8,128)} %broadcast_in_dim.49, s32[144]{0:T(256)S(1)} %bitcast.39, f32[144]{0:T(256)S(1)} %bitcast.45), kind=kCustom, calls=%fused_computation.1 | custom fusion | bytes 2880 | tf_op jit(solution)/shard_map/scatter | solution.py:48
  37.9 6.4 %all-to-all-start = ((f32[8,1,36]{2,1,0:T(1,128)}), f32[8,1,36]{2,1,0:T(1,128)S(1)}, u32[]{:S(2)}, u32[]{:S(2)}) async-start(f32[8,1,36]{2,1,0:T(1,128)} %bitcast.15), calls=%async_computation | async-start | bytes 8192 | tf_op jit(solution)/shard_map/all_to_all | solution.py:58
  44.4 0.0 copy-done.2
  44.4 0.1 fusion.6
  44.5 0.1 fusion.7
  44.6 123.4 %all-gather.2.cloned.1.call-done = f32[4608,1024]{1,0:T(8,128)} async-done(((f32[144,1024]{1,0:T(8,128)}), f32[4608,1024]{1,0:T(8,128)}) %all-gather.2.cloned.1.call-update) | async-done | bytes 18874384 | tf_op jit(solution)/shard_map/all_gather | solution.py:27
  168.0 23.8 %convolution_subtract_fusion = f32[144,4608]{1,0:T(8,128)S(1)} fusion(f32[144,1024]{1,0:T(8,128)} %fusion, f32[4608,1024]{1,0:T(8,128)} %all-gather.2.cloned.1.call-done, f32[1,144,4608]{2,1,0:T(8,128)} %param.9), kind=kOutput, calls=%fused_computation.4 | convolution fusion | flops 8154390528 | bytes 24772608 | tf_op jit(solution)/shard_map/dot_general | solution.py:25
  191.8 3.4 copy.17
  195.2 14.1 %gather_fusion = f32[4608,144]{1,0:T(8,128)} fusion(f32[144,4608]{0,1:T(8,128)} %copy.17, s32[5120]{0:T(1024)S(1)} %pad_clamp_fusion), kind=kCustom, calls=%fused_computation | custom fusion | bytes 5326848 | tf_op jit(solution)/shard_map/jit(_take)/gather | solution.py:9
  209.3 6.4 %multiply_bitcast_fusion = f32[144,4608]{0,1:T(8,128)} fusion(f32[4608,144]{1,0:T(8,128)} %gather_fusion, f32[4608]{0:T(1024)S(1)} %fusion.7, pred[4608]{0:T(1024)(128)(4,1)S(1)} %compare_and_fusion), kind=kLoop, calls=%fused_computation.5 | loop fusion | flops 1327104 | bytes 5331456 | tf_op jit(solution)/shard_map/mul | solution.py:9
  215.7 5.3 %copy.18 = f32[144,4608]{1,0:T(8,128)} copy(f32[144,4608]{0,1:T(8,128)} %multiply_bitcast_fusion) | data formatting | bytes 5308416 | tf_op jit(solution)/shard_map/mul | solution.py:9
  221.0 3.0 broadcast_in_dim.53
  224.0 39.2 %scatter_fusion.1 = f32[8,36,4608]{2,0,1:T(8,128)} fusion(f32[8,36,4608]{2,0,1:T(8,128)} %broadcast_in_dim.53, s32[144]{0:T(256)S(1)} %bitcast.40, f32[144,4608]{1,0:T(8,128)} %copy.18), kind=kCustom, calls=%fused_computation.2 | custom fusion | bytes 7963776 | tf_op jit(solution)/shard_map/scatter | solution.py:54
  263.3 8.1 %copy.19 = f32[8,36,4608]{2,1,0:T(8,128)} copy(f32[8,36,4608]{2,0,1:T(8,128)} %scatter_fusion.1) | data formatting | bytes 10616832 | tf_op jit(solution)/shard_map/scatter | solution.py:54
  271.4 0.0 copy-start.3
  271.4 0.0 all-to-all-done
  271.4 5.5 %all-to-all-start.1 = ((f32[8,36,4608]{2,1,0:T(8,128)}), f32[8,36,4608]{2,1,0:T(8,128)}, u32[]{:S(2)}, u32[]{:S(2)}) async-start(f32[8,36,4608]{2,1,0:T(8,128)} %copy.19), calls=%async_computation.1 | async-start | bytes 11796480 | tf_op jit(solution)/shard_map/all_to_all | solution.py:57
  276.9 0.0 copy-done.3
  277.0 0.1 select_n.81
  277.1 0.0 copy-start.1
  277.1 2.7 fusion.15
  279.9 64.2 %all-to-all-done.1 = f32[8,36,4608]{2,1,0:T(8,128)} async-done(((f32[8,36,4608]{2,1,0:T(8,128)}), f32[8,36,4608]{2,1,0:T(8,128)}, u32[]{:S(2)}, u32[]{:S(2)}) %all-to-all-start.1) | async-done | bytes 5308448 | tf_op jit(solution)/shard_map/all_to_all | solution.py:57
  344.1 5.6 %reshape.169 = f32[288,4608]{1,0:T(8,128)} reshape(f32[8,36,4608]{2,1,0:T(8,128)} %all-to-all-done.1) | data formatting | bytes 10616832 | tf_op jit(solution)/shard_map/reshape | solution.py:60
  349.7 10.6 %scatter_custom_fusion.2 = f32[144,4608]{1,0:T(8,128)} fusion(s32[288]{0:T(512)S(1)} %fusion.13, f32[288,4608]{1,0:T(8,128)} %reshape.169, f32[]{:T(128)} %constant.13.clone.1), kind=kCustom, calls=%fused_computation.8 | custom fusion | flops 1327104 | bytes 2654720 | tf_op jit(solution)/shard_map/scatter-add | solution.py:64
  360.2 0.0 copy-done.1
  (16 shorter events, 0.3 us)
Async XLA Ops:
  7.2 1.0 copy-start
  7.2 7.1 %copy-start.4 = (s32[1,144,1]{1,2,0:T(1,128)S(1)}, s32[1,144,1]{1,2,0:T(1,128)}, u32[]{:S(2)}) copy-start(s32[1,144,1]{1,2,0:T(1,128)} %param.14) | copy-start | bytes 1732
  7.2 7.9 %copy-start.5 = (s32[1,144]{1,0:T(1,128)S(1)}, s32[1,144]{1,0:T(1,128)}, u32[]{:S(2)}) copy-start(s32[1,144]{1,0:T(1,128)} %param.15) | copy-start | bytes 1732
  7.2 37.2 %copy-start.2 = (s32[1,4608]{1,0:T(1,128)S(1)}, s32[1,4608]{1,0:T(1,128)}, u32[]{:S(2)}) copy-start(s32[1,4608]{1,0:T(1,128)} %param.13) | copy-start | bytes 55300
  7.2 160.8 %all-gather.2.cloned.1.call-start = ((), (), s32[]{:S(2)}) async-start(), calls=%async_computation.2 | async-start | bytes 19464192 | tf_op jit(solution)/shard_map/all_gather | solution.py:27
  37.9 233.4 %all-to-all-start = ((f32[8,1,36]{2,1,0:T(1,128)}), f32[8,1,36]{2,1,0:T(1,128)S(1)}, u32[]{:S(2)}, u32[]{:S(2)}) async-start(f32[8,1,36]{2,1,0:T(1,128)} %bitcast.15), calls=%async_computation | async-start | bytes 8192 | tf_op jit(solution)/shard_map/all_to_all | solution.py:58
  271.4 5.5 %copy-start.3 = (f32[1,4608]{1,0:T(1,128)S(1)}, f32[1,4608]{1,0:T(1,128)}, u32[]{:S(2)}) copy-start(f32[1,4608]{1,0:T(1,128)} %param.11) | copy-start | bytes 55300
  271.4 72.7 %all-to-all-start.1 = ((f32[8,36,4608]{2,1,0:T(8,128)}), f32[8,36,4608]{2,1,0:T(8,128)}, u32[]{:S(2)}, u32[]{:S(2)}) async-start(f32[8,36,4608]{2,1,0:T(8,128)} %copy.19), calls=%async_computation.1 | async-start | bytes 11796480 | tf_op jit(solution)/shard_map/all_to_all | solution.py:57
  277.1 83.1 %copy-start.1 = (bf16[1,144,1024]{2,1,0:T(8,128)(2,1)S(1)}, bf16[1,144,1024]{2,1,0:T(8,128)(2,1)}, u32[]{:S(2)}) copy-start(bf16[1,144,1024]{2,1,0:T(8,128)(2,1)} %param.8) | copy-start | bytes 884740
Sparse Core Ops, SparseCore 0:
  13.7 154.2 all-gather.1
where the time goes:
time: 369 us; the launch traced here: 367 us
  waiting for transfers between devices  188 us (51%)
  local copies, waits for them, and re-layouts  103 us (28%)
  matrix products  31.9 us (9%)
  other arithmetic  18 us (5%)
  between operations  14.8 us (4%)
  starting transfers between devices  12 us (3%)
    all_gather x1, waiting for transfers between devices, on_device(): lax.all_gather(factor, 'grp', axis=0, tiled=True)  123 us
    all_to_all x1, waiting for transfers between devices, on_device(): lax.all_to_all(bucket, 'front', split_axis=0, concat_axis=0, tiled=True)  64.2 us
    scatter x2, local copies, waits for them, and re-layouts, on_device(): bucket = jnp.zeros((fronts, capacity, col_count), jnp.float32).at[dest_li...  47.3 us
    dot_general x1, matrix products, on_device(): lax.dot_general(factor, lax.all_gather(factor, 'grp', axis=0, tiled=True)...  23.8 us
    scatter x1, local copies, waits for them, and re-layouts, on_device(): row_tags = jnp.full((fronts, capacity), -1.0, jnp.float32).at[dest_live,...  22.1 us
    gather x1, local copies, waits for them, and re-layouts, place_columns(): return jnp.take(rows, source, axis=1) * keep_cols[None, :]  14.1 us
    scatter-add x1, other arithmetic, on_device(): jnp.zeros((row_count, col_count), jnp.float32).at[target_row]  10.6 us
  transfers between devices with their start and end apart: 3, of which 2 were waited for; matrix products, arithmetic and copies ran while one was open for 35% of the time, Pallas kernels for 0%

commit v1 on v0

v1 whole, which is shorter than its diff:
```python
import jax
import jax.numpy as jnp
from jax import lax
from jax.sharding import PartitionSpec as P

HIGHEST = lax.Precision.HIGHEST


def bf16_terms(x):
    high = lax.reduce_precision(x, 8, 7)
    rest = x - high
    middle = lax.reduce_precision(rest, 8, 7)
    low = rest - middle
    return [t.astype(jnp.bfloat16) for t in (high, middle, low)]


def on_device(
    panel_block, trailing, inverse, weights, live_size, column_source, destination, row_offset
):
    row_count = trailing.shape[1]
    col_count = trailing.shape[2]
    fronts = lax.axis_size("front")
    capacity = max(2, 2 * row_count // fronts)
    slots = fronts * capacity
    trail_rows = trailing[0]
    inverse_rows = inverse[0]
    live_count = live_size[0]
    panel_all = lax.all_gather(panel_block[0], "grp", axis=0, tiled=True)
    panel_f32 = panel_block[0].astype(jnp.float32)
    factor = jnp.dot(panel_f32, inverse_rows.T, precision=HIGHEST)
    twice = jnp.dot(factor, inverse_rows, precision=HIGHEST)

    rows = jnp.arange(row_count, dtype=jnp.int32)
    live_rows = lax.axis_index("grp") * row_count + rows < live_count
    dest_front = jnp.where(live_rows, destination[0, :, 0], -1)
    earlier = (dest_front[:, None] == dest_front[None, :]) & (rows[None, :] < rows[:, None])
    slot_index = jnp.sum(earlier.astype(jnp.int32), axis=1)
    flat_slot = jnp.where(live_rows, dest_front * capacity + slot_index, -1)
    place = flat_slot[None, :] == jnp.arange(slots, dtype=jnp.int32)[:, None]
    row_tags = jnp.sum(jnp.where(place, row_offset[0][None, :] + 1, 0), axis=1) - 1
    row_tags = row_tags.astype(jnp.float32).reshape(fronts, capacity)
    received_tags = lax.all_to_all(row_tags, "front", split_axis=0, concat_axis=0, tiled=True)
    targets = received_tags.reshape(slots).astype(jnp.int32)
    land = (targets[None, :] == rows[:, None]).astype(jnp.float32)

    source = column_source[0]
    keep = (source < live_count).astype(jnp.float32)
    trail_permuted = jnp.take(trail_rows, source, axis=1)
    kept_weights = jnp.take(weights[0], source) * keep

    update = sum(
        lax.dot_general(
            term, panel_all, (((1,), (1,)), ((), ())), preferred_element_type=jnp.float32
        )
        for term in bf16_terms(twice)
    )
    permuted = (trail_permuted - jnp.take(update, source, axis=1)) * keep[None, :]
    checksum = jnp.dot(permuted, kept_weights, precision=HIGHEST)
    bucket = jnp.dot(place.astype(jnp.float32), permuted, precision=HIGHEST)
    received = lax.all_to_all(
        bucket.reshape(fronts, capacity, col_count), "front", split_axis=0, concat_axis=0, tiled=True
    )
    ancestor = jnp.dot(land, received.reshape(slots, col_count), precision=HIGHEST)
    return (factor[None], checksum[None], ancestor[None])


def solution(mesh):
    placed = (
        P("front", "grp", None),
        P("front", "grp", None),
        P("front", None, None),
        P("front", None),
        P("front"),
        P("front", None),
        P("front", "grp", None),
        P("front", "grp"),
    )
    return jax.shard_map(
        on_device,
        mesh=mesh,
        in_specs=placed,
        out_specs=(P("front", "grp", None), P("front", "grp"), P("front", "grp", None)),
        check_vma=False,
    )
```

time: 369 us -> 258 us (0.70)
  waiting for transfers between devices: 188 us -> 108 us
  local copies, waits for them, and re-layouts: 103 us -> 73.7 us
  other arithmetic: 18 us -> 2.64 us
  matrix products: 31.9 us -> 46.2 us
    scatter x3 -> x0, local copies, waits for them, and re-layouts: 69.4 us -> none  [the longest x2 47.3 us: on_device(): bucket = jnp.zeros((fronts, capacity, col_count), jnp.float32).at[dest_li...]
    all_gather x1, waiting for transfers between devices: 123 us -> 71.8 us  [on_device(): panel_all = lax.all_gather(panel_block[0], 'grp', axis=0, tiled=True)]
    gather x1 -> x3, local copies, waits for them, and re-layouts: 14.1 us -> 52.4 us  [the longest x1 24.1 us: on_device(): kept_weights = jnp.take(weights[0], source) * keep]
    all_to_all x1, waiting for transfers between devices: 64.2 us -> 35.3 us  [on_device(): lax.all_to_all(bucket.reshape(fronts, capacity, col_count), 'front', spli...]
    dot_general x3 -> x8, matrix products: 31.9 us -> 46.2 us  [the longest x3 13.7 us: on_device(): lax.dot_general(term, panel_all, (((1,), (1,)), ((), ())), preferred_elem...]
    scatter-add x1 -> x0, other arithmetic: 10.6 us -> none  [on_device(): jnp.zeros((row_count, col_count), jnp.float32).at[target_row]]
    mul x3 -> x2, other arithmetic: 6.47 us -> 0.07 us  [the longest x1 0.05 us: on_device(): (trail_permuted - jnp.take(update, source, axis=1)) * keep[None, :]]
    reshape x1 -> x2, local copies, waits for them, and re-layouts: 5.58 us -> 11.2 us  [the longest x1 5.64 us: on_device(): received.reshape(slots, col_count)]
  transfers between devices with their start and end apart: 3 -> 3, of which waited for: 2 -> 2; matrix products, arithmetic and copies ran while one was open for 35% -> 42% of each run, Pallas kernels for 0% -> 0%
where the time goes in v1:
time: 258 us; the launch traced here: 257 us
  waiting for transfers between devices  108 us (42%)
  local copies, waits for them, and re-layouts  73.7 us (29%)
  matrix products  46.2 us (18%)
  between operations  14.8 us (6%)
  starting transfers between devices  12.2 us (5%)
  other arithmetic  2.64 us (1%)
    all_gather x1, waiting for transfers between devices, on_device(): panel_all = lax.all_gather(panel_block[0], 'grp', axis=0, tiled=True)  71.8 us
    all_to_all x1, waiting for transfers between devices, on_device(): lax.all_to_all(bucket.reshape(fronts, capacity, col_count), 'front', spli...  35.3 us
    gather x1, local copies, waits for them, and re-layouts, on_device(): kept_weights = jnp.take(weights[0], source) * keep  24.1 us
    gather x1, local copies, waits for them, and re-layouts, on_device(): trail_permuted = jnp.take(trail_rows, source, axis=1)  14.1 us
    gather x1, local copies, waits for them, and re-layouts, on_device(): jnp.take(update, source, axis=1)  14.1 us
    dot_general x3, matrix products, on_device(): lax.dot_general(term, panel_all, (((1,), (1,)), ((), ())), preferred_elem...  13.7 us
    dot_general x1, matrix products, on_device(): bucket = jnp.dot(place.astype(jnp.float32), permuted, precision=HIGHEST)  10.9 us
    dot_general x1, matrix products, on_device(): checksum = jnp.dot(permuted, kept_weights, precision=HIGHEST)  7.47 us
  transfers between devices with their start and end apart: 3, of which 2 were waited for; matrix products, arithmetic and copies ran while one was open for 42% of the time, Pallas kernels for 0%

profile of v1, /device:TPU:1, one launch (start us, length us, event | category | flops | bytes accessed | tf_op | source)
XLA Modules:
  0.0 257.4 jit_solution(17557925677657125797)
XLA Ops:
  7.2 0.0 copy-start
  7.2 0.0 copy-start.5
  7.2 0.0 all-gather.3.cloned.1.call-start
  7.2 0.7 all-gather.3.cloned.1.call-update
  8.6 0.7 fusion.28
  9.3 0.2 convert_reduce_fusion
  9.5 0.7 broadcast_add_fusion
  10.1 0.7 add_select_fusion
  10.8 0.1 select_reduce_fusion
  11.0 0.7 convert_element_type.46
  11.6 6.5 %all-to-all-start = ((f32[8,1,36]{2,1,0:T(1,128)}), f32[8,1,36]{2,1,0:T(1,128)S(1)}, u32[]{:S(2)}, u32[]{:S(2)}) async-start(f32[8,1,36]{2,1,0:T(1,128)} %convert_element_type.46), calls=%async_computation | async-start | bytes 8192 | tf_op jit(solution)/shard_map/all_to_all | solution.py:42
  18.1 5.1 %copy.15 = f32[1,144,4608]{1,2,0:T(8,128)} copy(f32[1,144,4608]{2,1,0:T(8,128)} %param.11) | data formatting | bytes 5308416 | tf_op args[1]
  23.2 0.0 copy-done.5
  23.3 0.0 copy-start.4
  23.3 14.1 %gather_fusion.1 = f32[4608,144]{1,0:T(8,128)} fusion(f32[144,4608]{0,1:T(8,128)} %bitcast.46, s32[5120]{0:T(1024)S(1)} %pad_clamp_fusion.1), kind=kCustom, calls=%fused_computation.clone | custom fusion | bytes 5326848 | tf_op jit(solution)/shard_map/jit(_take)/gather | solution.py:48
  37.4 0.0 copy-start.2
  37.4 0.1 fusion.27
  37.5 0.0 copy-done.4
  37.5 4.8 %fusion.15 = f32[144,1024]{1,0:T(8,128)S(1)} fusion(f32[1,1024,1024]{2,1,0:T(8,128)} %param.12, bf16[1,144,1024]{2,1,0:T(8,128)(2,1)S(1)} %copy-done.4), kind=kOutput, calls=%fused_computation.16 | convolution fusion | flops 1811939328 | bytes 5079040 | tf_op jit(solution)/shard_map/dot_general | solution.py:30
  42.3 0.0 copy-start.3
  42.3 0.8 copy-done.3
  43.1 0.0 copy-done.2
  43.1 2.6 fusion.13
  45.7 71.8 %all-gather.3.cloned.1.call-done = bf16[1,4608,1024]{2,1,0:T(8,128)(2,1)} async-done(((bf16[1,144,1024]{2,1,0:T(8,128)(2,1)}), bf16[1,4608,1024]{2,1,0:T(8,128)(2,1)}) %all-gather.3.cloned.1.call-update) | async-done | bytes 9437200 | tf_op jit(solution)/shard_map/all_gather | solution.py:28
  117.6 0.0 copy-start.1
  117.6 7.1 %fusion = f32[144,4608]{1,0:T(8,128)S(1)} fusion(bf16[1,4608,1024]{2,1,0:T(8,128)(2,1)} %all-gather.3.cloned.1.call-done, f32[144,1024]{1,0:T(8,128)S(1)} %fusion.13), kind=kOutput, calls=%fused_computation.3 | convolution fusion | flops 1359691776 | bytes 12681216 | tf_op jit(solution)/shard_map/dot_general | solution.py:52
  124.7 0.0 copy-done.1
  124.7 3.3 %fusion.2 = f32[144,4608]{1,0:T(8,128)S(1)} fusion(bf16[1,4608,1024]{2,1,0:T(8,128)(2,1)S(1)} %copy-done.1, f32[144,1024]{1,0:T(8,128)S(1)} %fusion.13), kind=kOutput, calls=%fused_computation.5 | convolution fusion | flops 1359544320 | bytes 12681216 | tf_op jit(solution)/shard_map/dot_general | solution.py:52
  127.9 3.3 %fusion.9 = f32[144,4608]{1,0:T(8,128)S(1)} fusion(f32[144,4608]{1,0:T(8,128)S(1)} %fusion, f32[144,4608]{1,0:T(8,128)S(1)} %fusion.2, bf16[1,4608,1024]{2,1,0:T(8,128)(2,1)S(1)} %copy-done.1, f32[144,1024]{1,0:T(8,128)S(1)} %fusion.13), kind=kOutput, calls=%fused_computation.11 | convolution fusion | flops 1360576512 | bytes 17989632 | tf_op jit(solution)/shard_map/dot_general | solution.py:52
  131.3 3.4 %copy.16 = f32[144,4608]{0,1:T(8,128)} copy(f32[144,4608]{1,0:T(8,128)S(1)} %fusion.9) | data formatting | bytes 5308416 | tf_op jit(solution)/shard_map/add | solution.py:51
  134.6 14.1 %gather_fusion.2 = f32[4608,144]{1,0:T(8,128)} fusion(f32[144,4608]{0,1:T(8,128)} %copy.16, s32[5120]{0:T(1024)S(1)} %pad_clamp_fusion.1), kind=kCustom, calls=%fused_computation.1.clone | custom fusion | bytes 5326848 | tf_op jit(solution)/shard_map/jit(_take)/gather | solution.py:57
  148.8 10.9 %fusion.22 = f32[288,4608]{1,0:T(8,128)} fusion(s32[144]{0:T(256)S(1)} %add_select_fusion, f32[4608,144]{1,0:T(8,128)} %gather_fusion.2, f32[4608,144]{1,0:T(8,128)} %gather_fusion.1, f32[4608]{0:T(1024)S(1)} %fusion.27, pred[4608]{0:T(1024)(128)(4,1)S(1)} %compare_and_fusion), kind=kOutput, calls=%fused_computation.31 | convolution fusion | flops 2295972864 | bytes 10640448 | tf_op jit(solution)/shard_map/dot_general | solution.py:59
  159.7 5.6 %reshape.109 = f32[8,36,4608]{2,1,0:T(8,128)} reshape(f32[288,4608]{1,0:T(8,128)} %fusion.22) | data formatting | bytes 10616832 | tf_op jit(solution)/shard_map/reshape | solution.py:61
  165.3 0.0 all-to-all-done
  165.3 5.7 %all-to-all-start.1 = ((f32[8,36,4608]{2,1,0:T(8,128)}), f32[8,36,4608]{2,1,0:T(8,128)}, u32[]{:S(2)}, u32[]{:S(2)}) async-start(f32[8,36,4608]{2,1,0:T(8,128)} %reshape.109), calls=%async_computation.1 | async-start | bytes 11796480 | tf_op jit(solution)/shard_map/all_to_all | solution.py:60
  171.0 0.0 copy-done
  171.0 0.1 fusion.26
  171.1 24.1 %gather_fusion = f32[4608]{0:T(1024)S(1)} fusion(f32[4608]{0:T(1024)S(1)} %reduce.2, s32[5120]{0:T(1024)S(1)} %pad_clamp_fusion), kind=kCustom, calls=%fused_computation.2 | custom fusion | bytes 55296 | tf_op jit(solution)/shard_map/jit(_take)/gather | solution.py:49
  195.2 0.1 convert_element_type.48
  195.3 7.5 %fusion.30 = f32[1,144]{1,0:T(1,128)} fusion(f32[4608,1]{0,1:T(1,128)S(1)} %reshape.143, f32[4608,144]{1,0:T(8,128)} %gather_fusion.2, f32[4608,144]{1,0:T(8,128)} %gather_fusion.1, f32[4608]{0:T(1024)S(1)} %fusion.27, pred[4608]{0:T(1024)(128)(4,1)S(1)} %compare_and_fusion), kind=kOutput, calls=%fused_computation.49 | convolution fusion | flops 10616832 | bytes 5350464 | tf_op jit(solution)/shard_map/dot_general | solution.py:58
  202.8 35.3 %all-to-all-done.1 = f32[8,36,4608]{2,1,0:T(8,128)} async-done(((f32[8,36,4608]{2,1,0:T(8,128)}), f32[8,36,4608]{2,1,0:T(8,128)}, u32[]{:S(2)}, u32[]{:S(2)}) %all-to-all-start.1) | async-done | bytes 5308448 | tf_op jit(solution)/shard_map/all_to_all | solution.py:60
  238.1 5.6 %reshape.110 = f32[288,4608]{1,0:T(8,128)} reshape(f32[8,36,4608]{2,1,0:T(8,128)} %all-to-all-done.1) | data formatting | bytes 10616832 | tf_op jit(solution)/shard_map/reshape | solution.py:63
  243.8 6.8 %convolution_bitcast_fusion = f32[1,144,4608]{2,1,0:T(8,128)} fusion(f32[288,4608]{1,0:T(8,128)} %reshape.110, s32[288]{0:T(512)S(1)} %convert_element_type.48), kind=kOutput, calls=%fused_computation.9 | convolution fusion | flops 2293277184 | bytes 7963776 | tf_op jit(solution)/shard_map/dot_general | solution.py:63
  (10 shorter events, 0.2 us)
Async XLA Ops:
  7.2 163.8 %copy-start = (f32[1,4608]{1,0:T(1,128)S(1)}, f32[1,4608]{1,0:T(1,128)}, u32[]{:S(2)}) copy-start(f32[1,4608]{1,0:T(1,128)} %param.13) | copy-start | bytes 55300
  7.2 16.0 %copy-start.5 = (s32[1,4608]{1,0:T(1,128)S(1)}, s32[1,4608]{1,0:T(1,128)}, u32[]{:S(2)}) copy-start(s32[1,4608]{1,0:T(1,128)} %param.15) | copy-start | bytes 55300
  7.2 110.4 %all-gather.3.cloned.1.call-start = ((), (), s32[]{:S(2)}) async-start(), calls=%async_computation.2 | async-start | bytes 9732096 | tf_op jit(solution)/shard_map/all_gather | solution.py:28
  11.6 153.6 %all-to-all-start = ((f32[8,1,36]{2,1,0:T(1,128)}), f32[8,1,36]{2,1,0:T(1,128)S(1)}, u32[]{:S(2)}, u32[]{:S(2)}) async-start(f32[8,1,36]{2,1,0:T(1,128)} %convert_element_type.46), calls=%async_computation | async-start | bytes 8192 | tf_op jit(solution)/shard_map/all_to_all | solution.py:42
  23.3 14.2 %copy-start.4 = (bf16[1,144,1024]{2,1,0:T(8,128)(2,1)S(1)}, bf16[1,144,1024]{2,1,0:T(8,128)(2,1)}, u32[]{:S(2)}) copy-start(bf16[1,144,1024]{2,1,0:T(8,128)(2,1)} %param.10) | copy-start | bytes 884740
  37.4 5.7 %copy-start.2 = (f32[1,1024,1024]{2,1,0:T(8,128)S(1)}, f32[1,1024,1024]{2,1,0:T(8,128)}, u32[]{:S(2)}) copy-start(f32[1,1024,1024]{2,1,0:T(8,128)} %param.12) | copy-start | bytes 12582916
  42.3 0.8 copy-start.3
  117.6 7.1 %copy-start.1 = (bf16[1,4608,1024]{2,1,0:T(8,128)(2,1)S(1)}, bf16[1,4608,1024]{2,1,0:T(8,128)(2,1)}, u32[]{:S(2)}) copy-start(bf16[1,4608,1024]{2,1,0:T(8,128)(2,1)} %all-gather.3.cloned.1.call-done) | copy-start | bytes 28311556
  165.3 72.9 %all-to-all-start.1 = ((f32[8,36,4608]{2,1,0:T(8,128)}), f32[8,36,4608]{2,1,0:T(8,128)}, u32[]{:S(2)}, u32[]{:S(2)}) async-start(f32[8,36,4608]{2,1,0:T(8,128)} %reshape.109), calls=%async_computation.1 | async-start | bytes 11796480 | tf_op jit(solution)/shard_map/all_to_all | solution.py:60
Sparse Core Ops, SparseCore 0:
  10.6 106.9 all-gather.2

commit v2 on v1

v2 whole, which is shorter than its diff:
```python
import jax
import jax.numpy as jnp
from jax import lax
from jax.sharding import PartitionSpec as P

HIGHEST = lax.Precision.HIGHEST
PANEL_TOP = 0.1796875


def bf16_terms(x):
    high = lax.reduce_precision(x, 8, 7)
    rest = x - high
    middle = lax.reduce_precision(rest, 8, 7)
    low = rest - middle
    return [t.astype(jnp.bfloat16) for t in (high, middle, low)]


def dot_bf16(a, b):
    return jnp.dot(a, b, preferred_element_type=jnp.float32)


def on_device(
    panel_block, trailing, inverse, weights, live_size, column_source, destination, row_offset
):
    row_count = trailing.shape[1]
    col_count = trailing.shape[2]
    fronts = lax.axis_size("front")
    capacity = -(-(row_count // 4) // 8) * 8
    slots = fronts * capacity
    trail_rows = trailing[0]
    inverse_rows = inverse[0]
    live_count = live_size[0]
    source = column_source[0]
    panel_all = lax.all_gather(panel_block[0], "grp", axis=0, tiled=True)
    panel_f32 = panel_block[0].astype(jnp.float32)
    factor = jnp.dot(panel_f32, inverse_rows.T, precision=HIGHEST)
    twice = jnp.dot(factor, inverse_rows, precision=HIGHEST)

    bound = jnp.max(jnp.abs(trail_rows), axis=1) + PANEL_TOP * jnp.sum(jnp.abs(twice), axis=1)
    scale = lax.reduce_precision(jnp.clip(bound, 2.0**-100, 2.0**120), 8, 0)
    inverse_scale = lax.reduce_precision(1.0 / scale, 8, 0)

    rows = jnp.arange(row_count, dtype=jnp.int32)
    live_rows = lax.axis_index("grp") * row_count + rows < live_count
    dest_front = jnp.where(live_rows, destination[0, :, 0], -1)
    earlier = (dest_front[:, None] == dest_front[None, :]) & (rows[None, :] < rows[:, None])
    slot_index = jnp.sum(earlier.astype(jnp.int32), axis=1)
    flat_slot = jnp.where(live_rows, dest_front * capacity + slot_index, -1)
    place = flat_slot[None, :] == jnp.arange(slots, dtype=jnp.int32)[:, None]
    row_tags = jnp.sum(jnp.where(place, row_offset[0][None, :] + 1, 0), axis=1) - 1
    row_tags = row_tags.astype(jnp.float32).reshape(fronts, 1, capacity)
    row_scales = jnp.sum(jnp.where(place, scale[None, :], 0.0), axis=1).reshape(fronts, 1, capacity)
    received_tags = lax.all_to_all(
        jnp.concatenate([row_tags, row_scales], axis=1),
        "front", split_axis=0, concat_axis=0, tiled=True,
    )
    targets = received_tags[:, 0].reshape(slots).astype(jnp.int32)
    scales = received_tags[:, 1].reshape(slots)
    land = jnp.where(targets[None, :] == rows[:, None], scales[None, :], 0.0).astype(jnp.bfloat16)
    spread = jnp.where(place, inverse_scale[None, :], 0.0).astype(jnp.bfloat16)

    columns = jnp.arange(col_count, dtype=jnp.int32)
    keep = source < live_count
    masked_weights = jnp.where(columns < live_count, weights[0], 0.0)
    trail_permuted = jnp.take(trail_rows, source, axis=1)
    weight_terms = jnp.stack(bf16_terms(masked_weights))
    trail_sum = jnp.sum(trail_rows * masked_weights[None, :], axis=1)

    terms = jnp.concatenate(bf16_terms(twice)[:2], axis=0)
    panel_all, factor, twice, terms, trail_permuted, trail_sum, land, spread = (
        lax.optimization_barrier(
            (panel_all, factor, twice, terms, trail_permuted, trail_sum, land, spread)
        )
    )
    panel_permuted = jnp.take(panel_all, source, axis=0)
    update = lax.dot_general(
        terms, panel_permuted, (((1,), (1,)), ((), ())), preferred_element_type=jnp.float32
    )
    update = update[:row_count] + update[row_count:]
    permuted = jnp.where(keep[None, :], trail_permuted - update, 0.0)
    high, middle, _ = bf16_terms(permuted)
    bucket = (dot_bf16(spread, high) + dot_bf16(spread, middle)).astype(jnp.float16)
    bucket, panel_all = lax.optimization_barrier((bucket, panel_all))
    received = lax.all_to_all(
        bucket.reshape(fronts, capacity, col_count), "front", split_axis=0, concat_axis=0, tiled=True
    )
    weighted = jnp.sum(dot_bf16(weight_terms, panel_all), axis=0)
    checksum = trail_sum - jnp.sum(twice * weighted, axis=1)
    received = received.reshape(slots, col_count).astype(jnp.float32)
    high, middle, _ = bf16_terms(received)
    ancestor = dot_bf16(land, high) + dot_bf16(land, middle)
    return (factor[None], checksum[None], ancestor[None])


def solution(mesh):
    placed = (
        P("front", "grp", None),
        P("front", "grp", None),
        P("front", None, None),
        P("front", None),
        P("front"),
        P("front", None),
        P("front", "grp", None),
        P("front", "grp"),
    )
    return jax.shard_map(
        on_device,
        mesh=mesh,
        in_specs=placed,
        out_specs=(P("front", "grp", None), P("front", "grp"), P("front", "grp", None)),
        check_vma=False,
    )
```

time: 258 us -> 206 us (0.80)
  local copies, waits for them, and re-layouts: 73.7 us -> 50.6 us
  matrix products: 46.2 us -> 25.1 us
  waiting for transfers between devices: 108 us -> 92.9 us
  other arithmetic: 2.64 us -> 10.4 us
    dot_general x6, matrix products: 38.8 us -> 19.2 us  [the longest x5 12 us: dot_bf16(): return jnp.dot(a, b, preferred_element_type=jnp.float32)]
    gather x2 -> x1, local copies, waits for them, and re-layouts: 38.2 us -> 25.6 us  [on_device(): panel_permuted = jnp.take(panel_all, source, axis=0)]
    reshape x2 -> x1, local copies, waits for them, and re-layouts: 11.2 us -> 0.09 us  [on_device(): jnp.sum(jnp.where(place, scale[None, :], 0.0), axis=1)]
    all_gather x1, waiting for transfers between devices: 71.8 us -> 62.6 us  [on_device(): panel_all = lax.all_gather(panel_block[0], 'grp', axis=0, tiled=True)]
    all_to_all x1, waiting for transfers between devices: 35.3 us -> 29.6 us  [on_device(): lax.all_to_all(bucket.reshape(fronts, capacity, col_count), 'front', spli...]
    gather x1 -> x2, local copies, waits for them, and re-layouts: 14.1 us -> 19.5 us  [on_device(): trail_permuted = jnp.take(trail_rows, source, axis=1)]
    reduce_max x0 -> x1, other arithmetic: none -> 4.11 us  [on_device(): jnp.max(jnp.abs(trail_rows), axis=1)]
    add x1 -> x0, local copies, waits for them, and re-layouts: 3.37 us -> none  [on_device(): sum((lax.dot_general(term, panel_all, (((1,), (1,)), ((), ())), preferred...]
  transfers between devices with their start and end apart: 3 -> 3, of which waited for: 2 -> 2; matrix products, arithmetic and copies ran while one was open for 42% -> 22% of each run, Pallas kernels for 0% -> 0%
where the time goes in v2:
time: 206 us
  waiting for transfers between devices  92.9 us (45%)
  local copies, waits for them, and re-layouts  50.6 us (25%)
  matrix products  25.1 us (12%)
  between operations  14.9 us (7%)
  starting transfers between devices  12 us (6%)
  other arithmetic  10.4 us (5%)
    all_gather x1, waiting for transfers between devices, on_device(): panel_all = lax.all_gather(panel_block[0], 'grp', axis=0, tiled=True)  62.6 us
    all_to_all x1, waiting for transfers between devices, on_device(): lax.all_to_all(bucket.reshape(fronts, capacity, col_count), 'front', spli...  29.6 us
    gather x1, local copies, waits for them, and re-layouts, on_device(): panel_permuted = jnp.take(panel_all, source, axis=0)  25.6 us
    gather x2, local copies, waits for them, and re-layouts, on_device(): trail_permuted = jnp.take(trail_rows, source, axis=1)  19.5 us
    dot_general x5, matrix products, dot_bf16(): return jnp.dot(a, b, preferred_element_type=jnp.float32)  12 us
    dot_general x1, matrix products, on_device(): lax.dot_general(terms, panel_permuted, (((1,), (1,)), ((), ())), preferre...  7.17 us
    all_to_all x1, starting transfers between devices, on_device(): lax.all_to_all(jnp.concatenate([row_tags, row_scales], axis=1), 'front',...  6.47 us
    all_to_all x1, starting transfers between devices, on_device(): lax.all_to_all(bucket.reshape(fronts, capacity, col_count), 'front', spli...  5.47 us
  transfers between devices with their start and end apart: 3, of which 2 were waited for; matrix products, arithmetic and copies ran while one was open for 22% of the time, Pallas kernels for 0%

profile of v2, /device:TPU:1, one launch (start us, length us, event | category | flops | bytes accessed | tf_op | source)
XLA Modules:
  0.0 205.9 jit_solution(14632789426299940254)
XLA Ops:
  7.2 0.0 all-gather.3.cloned.1.call-start
  7.2 0.7 all-gather.3.cloned.1.call-update
  8.6 0.0 copy-start.9
  8.6 0.0 copy-start.8
  8.6 5.1 %copy.15 = f32[1,144,4608]{1,2,0:T(8,128)} copy(f32[1,144,4608]{2,1,0:T(8,128)} %param.9) | data formatting | bytes 5308416 | tf_op args[1]
  13.7 0.0 copy-done.9
  13.7 0.2 convert_reduce_fusion
  13.9 0.0 copy-done.8
  13.9 0.7 reduce-precision_convert_fusion.6
  14.6 4.1 %abs_reduce_fusion = (f32[144]{0:T(256)S(1)}, f32[144]{0:T(256)S(1)}) fusion(f32[1,144,4608]{1,2,0:T(8,128)} %copy.15, f32[4608]{0:T(1024)S(1)} %get-tuple-element.33), kind=kLoop, calls=%fused_computation.14 | loop fusion | flops 2653920 | bytes 2673792 | tf_op jit(solution)/shard_map/reduce_max | solution.py:39
  18.7 0.0 copy-done.3
  18.7 2.5 %fusion.10 = f32[144,1024]{1,0:T(8,128)S(1)} fusion(f32[1,1024,1024]{2,1,0:T(8,128)S(1)} %copy-done, bf16[1,144,1024]{2,1,0:T(8,128)(2,1)S(1)} %copy-done.3), kind=kOutput, calls=%fused_computation.18 | convolution fusion | flops 1811939328 | bytes 5079040 | tf_op jit(solution)/shard_map/dot_general | solution.py:36
  21.2 0.0 copy-start.1
  21.2 0.0 copy-start.10
  21.2 0.0 copy-start.4
  21.2 3.4 %abs_reduce_fusion.1 = (f32[144]{0:T(256)S(1)}, bf16[144,1024]{1,0:T(8,128)(2,1)S(1)}, bf16[144,1024]{1,0:T(8,128)(2,1)S(1)}, f32[144,1024]{1,0:T(8,128)}) fusion(f32[144,1024]{1,0:T(8,128)S(1)} %fusion.10, f32[1,1024,1024]{2,1,0:T(8,128)S(1)} %copy-done), kind=kOutput, calls=%fused_computation.37 | convolution fusion | flops 1812971392 | bytes 5964352 | tf_op jit(solution)/shard_map/dot_general | solution.py:37
  24.6 0.0 copy-done.1
  24.7 0.1 select_reduce_fusion
  24.8 0.1 reshape.128
  24.9 0.0 copy-done.10
  24.9 0.1 select_reduce_fusion.1
  25.0 0.1 convert_element_type.76
  25.1 0.6 pad_maximum_fusion.1
  25.7 6.5 %all-to-all-start = ((f32[8,2,40]{2,1,0:T(2,128)}), f32[8,2,40]{2,1,0:T(2,128)S(1)}, u32[]{:S(2)}, u32[]{:S(2)}) async-start(f32[8,2,40]{2,1,0:T(2,128)} %pad_maximum_fusion.1), calls=%async_computation | async-start | bytes 16384 | tf_op jit(solution)/shard_map/all_to_all | solution.py:53
  32.2 0.1 fusion.29
  32.3 14.2 %gather_fusion = f32[4608,144]{1,0:T(8,128)} fusion(f32[144,4608]{0,1:T(8,128)} %bitcast.41, s32[5120]{0:T(1024)S(1)} %pad_clamp_fusion), kind=kCustom, calls=%fused_computation | custom fusion | bytes 5326848 | tf_op jit(solution)/shard_map/jit(_take)/gather | solution.py:65
  46.5 5.3 %copy.16 = f32[4608,144]{0,1:T(8,128)} copy(f32[4608,144]{1,0:T(8,128)} %gather_fusion) | data formatting | bytes 5308416 | tf_op jit(solution)/shard_map/jit(_take)/gather | solution.py:65
  51.9 0.9 pad_maximum_fusion
  52.7 0.1 select_convert_fusion
  52.8 2.0 select_bitcast_fusion
  54.8 0.1 compare_reduce_fusion
  54.9 0.0 all-to-all-done
  54.9 0.1 convert_element_type.78
  55.0 0.1 broadcast_in_dim.120
  55.2 62.6 %all-gather.3.cloned.1.call-done = bf16[1,4608,1024]{2,1,0:T(8,128)(2,1)} async-done(((bf16[1,144,1024]{2,1,0:T(8,128)(2,1)}), bf16[1,4608,1024]{2,1,0:T(8,128)(2,1)}) %all-gather.3.cloned.1.call-update) | async-done | bytes 9437200 | tf_op jit(solution)/shard_map/all_gather | solution.py:34
  117.8 25.6 %gather_fusion.1 = bf16[4608,1024]{1,0:T(8,128)(2,1)} fusion(bf16[4608,1024]{1,0:T(8,128)(2,1)} %bitcast.39, s32[5120]{0:T(1024)S(1)} %pad_clamp_fusion), kind=kCustom, calls=%fused_computation.1 | custom fusion | bytes 18892800 | tf_op jit(solution)/shard_map/jit(_take)/gather | solution.py:75
  143.3 7.2 %fusion = f32[288,4608]{1,0:T(8,128)S(1)} fusion(bf16[288,1024]{1,0:T(8,128)(2,1)} %pad_maximum_fusion, bf16[4608,1024]{1,0:T(8,128)(2,1)} %gather_fusion.1, pred[4608]{0:T(1024)(128)(4,1)S(1)} %compare_and_fusion), kind=kOutput, calls=%fused_computation.2 | convolution fusion | flops 2722627584 | bytes 15340032 | tf_op jit(solution)/shard_map/dot_general | solution.py:76
  150.5 0.7 fusion.17
  151.2 1.0 fusion.19
  152.2 2.6 %fusion.3 = f16[320,4608]{1,0:T(8,128)(2,1)} fusion(f32[320,4608]{1,0:T(8,128)S(1)} %fusion.19, bf16[320,144]{0,1:T(8,128)(2,1)S(1)} %select_convert_fusion, f32[144,4608]{1,0:T(8,128)S(1)} %fusion.17), kind=kOutput, calls=%fused_computation.8 | convolution fusion | flops 430276608 | bytes 11593728 | tf_op jit(solution)/shard_map/dot_general | solution.py:19
  154.8 5.5 %all-to-all-start.1 = ((f16[8,40,4608]{2,1,0:T(8,128)(2,1)}), f16[8,40,4608]{2,1,0:T(8,128)(2,1)S(1)}, u32[]{:S(2)}, u32[]{:S(2)}) async-start(f16[8,40,4608]{2,1,0:T(8,128)(2,1)} %bitcast.44), calls=%async_computation.1 | async-start | bytes 5898240 | tf_op jit(solution)/shard_map/all_to_all | solution.py:84
  160.2 0.0 copy-done.5
  160.3 5.1 %convolution_reduce_fusion = f32[1024]{0:T(1024)S(1)} fusion(bf16[4608,1024]{1,0:T(8,128)(2,1)} %bitcast.40, bf16[1,4608]{1,0:T(2,128)(2,1)S(1)} %copy-done.7, bf16[1,4608]{1,0:T(2,128)(2,1)S(1)} %copy-done.6, bf16[1,4608]{1,0:T(2,128)(2,1)S(1)} %copy-done.5), kind=kOutput, calls=%fused_computation.30 | convolution fusion | flops 28396544 | bytes 9468928 | tf_op jit(solution)/shard_map/dot_general | solution.py:19
  165.4 0.1 multiply_reduce_fusion.1
  165.5 0.6 sub.34
  166.1 29.6 %all-to-all-done.1 = f16[8,40,4608]{2,1,0:T(8,128)(2,1)S(1)} async-done(((f16[8,40,4608]{2,1,0:T(8,128)(2,1)}), f16[8,40,4608]{2,1,0:T(8,128)(2,1)S(1)}, u32[]{:S(2)}, u32[]{:S(2)}) %all-to-all-start.1) | async-done | bytes 2949152 | tf_op jit(solution)/shard_map/all_to_all | solution.py:84
  195.7 0.9 fusion.13
  196.6 2.5 %fusion.4 = f32[1,144,4608]{2,1,0:T(8,128)} fusion(f32[144,4608]{1,0:T(8,128)S(1)} %fusion.13, bf16[144,320]{1,0:T(8,128)(2,1)S(1)} %select_convert_fusion.1, f16[320,4608]{1,0:T(8,128)(2,1)S(1)} %bitcast.43), kind=kOutput, calls=%fused_computation.10 | convolution fusion | flops 432709632 | bytes 8349696 | tf_op jit(solution)/shard_map/dot_general | solution.py:19
  (22 shorter events, 0.2 us)
Async XLA Ops:
  7.2 110.6 %all-gather.3.cloned.1.call-start = ((), (), s32[]{:S(2)}) async-start(), calls=%async_computation.2 | async-start | bytes 9732096 | tf_op jit(solution)/shard_map/all_gather | solution.py:34
  8.6 5.1 %copy-start.9 = (s32[1,144,1]{1,2,0:T(1,128)S(1)}, s32[1,144,1]{1,2,0:T(1,128)}, u32[]{:S(2)}) copy-start(s32[1,144,1]{1,2,0:T(1,128)} %param.14) | copy-start | bytes 1732
  8.6 5.3 %copy-start.8 = (f32[1,4608]{1,0:T(1,128)S(1)}, f32[1,4608]{1,0:T(1,128)}, u32[]{:S(2)}) copy-start(f32[1,4608]{1,0:T(1,128)} %param.11) | copy-start | bytes 55300
  13.7 5.0 %copy-start.3 = (bf16[1,144,1024]{2,1,0:T(8,128)(2,1)S(1)}, bf16[1,144,1024]{2,1,0:T(8,128)(2,1)}, u32[]{:S(2)}) copy-start(bf16[1,144,1024]{2,1,0:T(8,128)(2,1)} %param.8) | copy-start | bytes 884740
  13.7 5.0 %copy-start = (f32[1,1024,1024]{2,1,0:T(8,128)S(1)}, f32[1,1024,1024]{2,1,0:T(8,128)}, u32[]{:S(2)}) copy-start(f32[1,1024,1024]{2,1,0:T(8,128)} %param.10) | copy-start | bytes 12582916
  21.2 3.5 %copy-start.1 = (f32[144,1024]{1,0:T(8,128)}, f32[144,1024]{1,0:T(8,128)S(1)}, u32[]{:S(2)}) copy-start(f32[144,1024]{1,0:T(8,128)S(1)} %fusion.10) | copy-start | bytes 1769476
  21.2 3.7 %copy-start.10 = (s32[1,144]{1,0:T(1,128)S(1)}, s32[1,144]{1,0:T(1,128)}, u32[]{:S(2)}) copy-start(s32[1,144]{1,0:T(1,128)} %param.15) | copy-start | bytes 1732
  21.2 11.0 %copy-start.4 = (s32[1,4608]{1,0:T(1,128)S(1)}, s32[1,4608]{1,0:T(1,128)}, u32[]{:S(2)}) copy-start(s32[1,4608]{1,0:T(1,128)} %param.13) | copy-start | bytes 55300
  25.7 29.2 %all-to-all-start = ((f32[8,2,40]{2,1,0:T(2,128)}), f32[8,2,40]{2,1,0:T(2,128)S(1)}, u32[]{:S(2)}, u32[]{:S(2)}) async-start(f32[8,2,40]{2,1,0:T(2,128)} %pad_maximum_fusion.1), calls=%async_computation | async-start | bytes 16384 | tf_op jit(solution)/shard_map/all_to_all | solution.py:53
  154.8 5.5 %copy-start.5 = (bf16[1,4608]{1,0:T(2,128)(2,1)S(1)}, bf16[1,4608]{1,0:T(2,128)(2,1)}, u32[]{:S(2)}) copy-start(bf16[1,4608]{1,0:T(2,128)(2,1)} %get-tuple-element.30) | copy-start | bytes 27652
  154.8 5.5 %copy-start.6 = (bf16[1,4608]{1,0:T(2,128)(2,1)S(1)}, bf16[1,4608]{1,0:T(2,128)(2,1)}, u32[]{:S(2)}) copy-start(bf16[1,4608]{1,0:T(2,128)(2,1)} %get-tuple-element.31) | copy-start | bytes 27652
  154.8 5.5 %copy-start.7 = (bf16[1,4608]{1,0:T(2,128)(2,1)S(1)}, bf16[1,4608]{1,0:T(2,128)(2,1)}, u32[]{:S(2)}) copy-start(bf16[1,4608]{1,0:T(2,128)(2,1)} %get-tuple-element.32) | copy-start | bytes 27652
  154.8 40.9 %all-to-all-start.1 = ((f16[8,40,4608]{2,1,0:T(8,128)(2,1)}), f16[8,40,4608]{2,1,0:T(8,128)(2,1)S(1)}, u32[]{:S(2)}, u32[]{:S(2)}) async-start(f16[8,40,4608]{2,1,0:T(8,128)(2,1)} %bitcast.44), calls=%async_computation.1 | async-start | bytes 5898240 | tf_op jit(solution)/shard_map/all_to_all | solution.py:84
  160.3 5.1 %copy-start.2 = (f32[144,1024]{1,0:T(8,128)S(1)}, f32[144,1024]{1,0:T(8,128)}, u32[]{:S(2)}) copy-start(f32[144,1024]{1,0:T(8,128)} %get-tuple-element.15) | copy-start | bytes 1769476
Sparse Core Ops, SparseCore 0:
  10.6 107.1 all-gather.2

commit v3 on v2

--- a/solution.py
+++ b/solution.py
@@ -1,6 +1,11 @@
+import functools
+import heapq
+
 import jax
 import jax.numpy as jnp
 from jax import lax
+from jax.experimental import pallas as pl
+from jax.experimental.pallas import tpu as pltpu
 from jax.sharding import PartitionSpec as P
 
 HIGHEST = lax.Precision.HIGHEST
@@ -13,6 +18,124 @@
     middle = lax.reduce_precision(rest, 8, 7)
     low = rest - middle
     return [t.astype(jnp.bfloat16) for t in (high, middle, low)]
+
+
+RINGS = (4, 8)
+SHARES = ((1, 0, 0, 5), (0, 1, 5, 8))
+
+
+def gather_plan():
+    copies, steps, free, heap = [], [], {}, []
+    landed = {}
+
+    def send(now, share, phase, offset, hop, way):
+        axis = SHARES[share][phase]
+        span = SHARES[share][3] - SHARES[share][2]
+        size = span / 8 * (0.5 if hop == RINGS[axis] // 2 else 1.0)
+        link = (axis, way)
+        free[link] = max(now, free.get(link, 0.0)) + 6.3 * size
+        heapq.heappush(heap, (free[link] + 1.6, len(copies)))
+        copies.append((share, phase, offset, hop, way))
+
+    def forward(now, share, phase, offset, hop):
+        for way in (1, -1):
+            send(now, share, phase, offset, hop, way)
+
+    for phase in (0, 1):
+        for share in (0, 1):
+            forward(0.0, share, phase, 0, 1)
+    starts = len(copies)
+    while heap:
+        now, number = heapq.heappop(heap)
+        share, phase, offset, hop, way = copies[number]
+        half = RINGS[SHARES[share][phase]] // 2
+        first = len(copies)
+        if hop < half:
+            send(now, share, phase, offset, hop + 1, way)
+        if phase == 0:
+            place = -way * hop if hop < half else half
+            landed[share, place] = landed.get((share, place), 0) + 1
+            if hop < half or landed[share, place] == 2:
+                forward(now, share, 1, place, 1)
+        steps.append((number, range(first, len(copies))))
+    return copies, starts, steps
+
+
+def gather_kernel(plan, panel_ref, all_ref, send_sems, recv_sems, own_sem):
+    copies, starts, steps = plan
+    rows, width = panel_ref.shape
+    cut = rows * 5 // 9
+    me = lax.axis_index("grp")
+    here = (me // RINGS[1], me % RINGS[1])
+
+    def neighbour(axis, way):
+        there = list(here)
+        there[axis] = (here[axis] + way + RINGS[axis]) % RINGS[axis]
+        return {"grp": there[0] * RINGS[1] + there[1]}
+
+    def copy_of(number, arriving):
+        share, phase, offset, hop, way = copies[number]
+        first, second, begin, end = SHARES[share]
+        axis = SHARES[share][phase]
+        moved = -way * (hop if arriving else hop - 1)
+        spot = [None, None]
+        spot[first] = moved if phase == 0 else offset
+        spot[second] = 0 if phase == 0 else moved
+        own = spot == [0, 0]
+        spot = [(h + o + n) % n for h, o, n in zip(here, spot, RINGS)]
+        if hop < RINGS[axis] // 2:
+            part = pl.ds(0, rows)
+        else:
+            part = pl.ds(0, cut) if way == 1 else pl.ds(cut, rows - cut)
+        columns = pl.ds(begin * width // 8, (end - begin) * width // 8)
+        target = all_ref.at[spot[0], spot[1], part, columns]
+        return pltpu.make_async_remote_copy(
+            src_ref=panel_ref.at[part, columns] if own else target,
+            dst_ref=target,
+            send_sem=send_sems.at[number],
+            recv_sem=recv_sems.at[number],
+            device_id=neighbour(axis, way),
+            device_id_type=pl.DeviceIdType.MESH,
+        )
+
+    barrier = pltpu.get_barrier_semaphore()
+    for axis in (0, 1):
+        for way in (1, -1):
+            pl.semaphore_signal(
+                barrier, inc=1, device_id=neighbour(axis, way), device_id_type=pl.DeviceIdType.MESH
+            )
+    pl.semaphore_wait(barrier, 4)
+
+    for number in range(starts):
+        copy_of(number, False).start()
+    keep = pltpu.make_async_copy(panel_ref, all_ref.at[here[0], here[1]], own_sem)
+    keep.start()
+    for number, following in steps:
+        copy_of(number, True).wait_recv()
+        for later in following:
+            copy_of(later, False).start()
+    keep.wait()
+    for number in range(len(copies)):
+        copy_of(number, False).wait_send()
+
+
+def gather_panels(panel):
+    plan = gather_plan()
+    count = len(plan[0])
+    rows, width = panel.shape
+    gathered = pl.pallas_call(
+        functools.partial(gather_kernel, plan),
+        out_shape=jax.ShapeDtypeStruct((*RINGS, rows, width), panel.dtype),
+        in_specs=[pl.BlockSpec(memory_space=pltpu.VMEM)],
+        out_specs=pl.BlockSpec(memory_space=pl.ANY),
+        scratch_shapes=[
+            pltpu.SemaphoreType.DMA((count,)),
+            pltpu.SemaphoreType.DMA((count,)),
+            pltpu.SemaphoreType.DMA,
+        ],
+        compiler_params=pltpu.CompilerParams(collective_id=0, has_side_effects=True),
+    )(panel)
+    return gathered.reshape(RINGS[0] * RINGS[1] * rows, width)
 
 
 def dot_bf16(a, b):
@@ -31,7 +154,7 @@
     inverse_rows = inverse[0]
     live_count = live_size[0]
     source = column_source[0]
-    panel_all = lax.all_gather(panel_block[0], "grp", axis=0, tiled=True)
+    panel_all = gather_panels(panel_block[0])
     panel_f32 = panel_block[0].astype(jnp.float32)
     factor = jnp.dot(panel_f32, inverse_rows.T, precision=HIGHEST)
     twice = jnp.dot(factor, inverse_rows, precision=HIGHEST)
@@ -62,30 +185,20 @@
     columns = jnp.arange(col_count, dtype=jnp.int32)
     keep = source < live_count
     masked_weights = jnp.where(columns < live_count, weights[0], 0.0)
-    trail_permuted = jnp.take(trail_rows, source, axis=1)
-    weight_terms = jnp.stack(bf16_terms(masked_weights))
-    trail_sum = jnp.sum(trail_rows * masked_weights[None, :], axis=1)
 
     terms = jnp.concatenate(bf16_terms(twice)[:2], axis=0)
-    panel_all, factor, twice, terms, trail_permuted, trail_sum, land, spread = (
-        lax.optimization_barrier(
-            (panel_all, factor, twice, terms, trail_permuted, trail_sum, land, spread)
-        )
-    )
-    panel_permuted = jnp.take(panel_all, source, axis=0)
     update = lax.dot_general(
-        terms, panel_permuted, (((1,), (1,)), ((), ())), preferred_element_type=jnp.float32
-    )
-    update = update[:row_count] + update[row_count:]
-    permuted = jnp.where(keep[None, :], trail_permuted - update, 0.0)
+        terms, panel_all, (((1,), (1,)), ((), ())), preferred_element_type=jnp.float32
+    )
+    schur = trail_rows - (update[:row_count] + update[row_count:])
+    permuted = jnp.where(keep[None, :], jnp.take(schur, source, axis=1), 0.0)
     high, middle, _ = bf16_terms(permuted)
     bucket = (dot_bf16(spread, high) + dot_bf16(spread, middle)).astype(jnp.float16)
-    bucket, panel_all = lax.optimization_barrier((bucket, panel_all))
+    bucket, schur = lax.optimization_barrier((bucket, schur))
     received = lax.all_to_all(
         bucket.reshape(fronts, capacity, col_count), "front", split_axis=0, concat_axis=0, tiled=True
     )
-    weighted = jnp.sum(dot_bf16(weight_terms, panel_all), axis=0)
-    checksum = trail_sum - jnp.sum(twice * weighted, axis=1)
+    checksum = jnp.sum(schur * masked_weights[None, :], axis=1)
     received = received.reshape(slots, col_count).astype(jnp.float32)
     high, middle, _ = bf16_terms(received)
     ancestor = dot_bf16(land, high) + dot_bf16(land, middle)

time: 206 us -> 162 us (0.79)
  Pallas kernels: 0 us -> 64.8 us
  waiting for transfers between devices: 92.9 us -> 32.6 us
  local copies, waits for them, and re-layouts: 50.6 us -> 17.9 us
  between operations: 14.9 us -> 1.48 us
  other arithmetic: 10.4 us -> 5.77 us
  matrix products: 25.1 us -> 27.9 us
    pallas_call x0 -> x1, Pallas kernels: none -> 64.8 us  [gather_panels(): pl.pallas_call(functools.partial(gather_kernel, plan), out_shape=jax.Shap...]
    all_gather x1 -> x0, waiting for transfers between devices: 62.6 us -> none  [on_device(): panel_all = lax.all_gather(panel_block[0], 'grp', axis=0, tiled=True)]
    gather x3 -> x1, local copies, waits for them, and re-layouts: 45.1 us -> 14.2 us  [on_device(): permuted = jnp.where(keep[None, :], jnp.take(schur, source, axis=1), 0.0)]
    unnamed x23 -> x18, local copies, waits for them, and re-layouts: 5.13 us -> 0.05 us
    reduce_max x1, other arithmetic: 4.11 us -> 0.61 us  [on_device(): jnp.max(jnp.abs(trail_rows), axis=1)]
    sub x0 -> x1, local copies, waits for them, and re-layouts: none -> 3.36 us  [on_device(): schur = trail_rows - (update[:row_count] + update[row_count:])]
    all_to_all x1, waiting for transfers between devices: 29.6 us -> 32.6 us  [on_device(): lax.all_to_all(bucket.reshape(fronts, capacity, col_count), 'front', spli...]
    dot_general x5 -> x4, matrix products: 12 us -> 14.6 us  [dot_bf16(): return jnp.dot(a, b, preferred_element_type=jnp.float32)]
  transfers between devices with their start and end apart: 3 -> 2, of which waited for: 2 -> 1; matrix products, arithmetic and copies ran while one was open for 22% -> 20% of each run, Pallas kernels for 0% -> 0%
where the time goes in v3:
time: 162 us
  Pallas kernels  64.8 us (40%)
  waiting for transfers between devices  32.6 us (20%)
  matrix products  27.9 us (17%)
  local copies, waits for them, and re-layouts  17.9 us (11%)
  starting transfers between devices  11.2 us (7%)
  other arithmetic  5.77 us (4%)
    pallas_call x1, Pallas kernels, gather_panels(): pl.pallas_call(functools.partial(gather_kernel, plan), out_shape=jax.Shap...  64.8 us
    all_to_all x1, waiting for transfers between devices, on_device(): lax.all_to_all(bucket.reshape(fronts, capacity, col_count), 'front', spli...  32.6 us
    dot_general x4, matrix products, dot_bf16(): return jnp.dot(a, b, preferred_element_type=jnp.float32)  14.6 us
    gather x1, local copies, waits for them, and re-layouts, on_device(): permuted = jnp.where(keep[None, :], jnp.take(schur, source, axis=1), 0.0)  14.2 us
    all_to_all x1, starting transfers between devices, on_device(): lax.all_to_all(jnp.concatenate([row_tags, row_scales], axis=1), 'front',...  6.28 us
    dot_general x1, matrix products, on_device(): lax.dot_general(terms, panel_all, (((1,), (1,)), ((), ())), preferred_ele...  5.69 us
    dot_general x1, matrix products, on_device(): factor = jnp.dot(panel_f32, inverse_rows.T, precision=HIGHEST)  4.95 us
    all_to_all x1, starting transfers between devices, on_device(): lax.all_to_all(bucket.reshape(fronts, capacity, col_count), 'front', spli...  4.93 us
  transfers between devices with their start and end apart: 2, of which 1 were waited for; matrix products, arithmetic and copies ran while one was open for 20% of the time, Pallas kernels for 0%

profile of v3, /device:TPU:1, one launch (start us, length us, event | category | flops | bytes accessed | tf_op | source)
XLA Modules:
  0.0 161.7 jit_solution(12886184864740535318)
XLA Ops:
  1.3 0.0 copy-start.2
  1.3 0.8 fusion.46
  2.1 0.2 convert_reduce_fusion
  2.3 4.9 %fusion.8 = f32[144,1024]{1,0:T(8,128)S(1)} fusion(f32[1,1024,1024]{2,1,0:T(8,128)} %param.10, bf16[1,144,1024]{2,1,0:T(8,128)(2,1)} %param.8), kind=kOutput, calls=%fused_computation.16 | convolution fusion | flops 1811939328 | bytes 5079040 | tf_op jit(solution)/shard_map/dot_general | solution.py:159
  7.3 0.0 copy-done.2
  7.3 0.0 copy-start.4
  7.3 2.7 %abs_reduce_fusion = (f32[144]{0:T(256)S(1)}, bf16[144,1024]{1,0:T(8,128)(2,1)S(1)}, bf16[144,1024]{1,0:T(8,128)(2,1)S(1)}) fusion(f32[144,1024]{1,0:T(8,128)S(1)} %fusion.8, f32[1,1024,1024]{2,1,0:T(8,128)S(1)} %copy-done.2), kind=kOutput, calls=%fused_computation.41 | convolution fusion | flops 1812971392 | bytes 5374528 | tf_op jit(solution)/shard_map/dot_general | solution.py:160
  10.0 0.0 copy-start.7
  10.0 64.8 %shard_map.103 = bf16[4,8,144,1024]{3,2,1,0:T(8,128)(2,1)} custom-call(bf16[144,1024]{1,0:T(8,128)(2,1)} %bitcast.44), custom_call_target="tpu_custom_call" | custom-call | tf_op jit(solution)/shard_map/pallas_call | solution.py:126
  74.8 0.0 copy-done.4
  74.8 0.0 copy-done.7
  74.8 0.0 copy-start.3
  74.8 5.7 %fusion.26 = f32[288,4608]{1,0:T(8,128)S(1)} fusion(bf16[4608,1024]{1,0:T(8,128)(2,1)} %bitcast.42, bf16[144,1024]{1,0:T(8,128)(2,1)S(1)} %get-tuple-element.12, bf16[144,1024]{1,0:T(8,128)(2,1)S(1)} %get-tuple-element.13), kind=kOutput, calls=%fused_computation.37 | convolution fusion | flops 2719088640 | bytes 15335424 | tf_op jit(solution)/shard_map/dot_general | solution.py:190
  80.5 0.0 copy-done.3
  80.5 0.0 copy-start.8
  80.5 0.6 fusion.13
  81.1 0.0 copy-start.1
  81.2 0.0 copy-start.5
  81.2 0.1 select_reduce_fusion
  81.3 0.1 reshape.128
  81.4 0.0 copy-done.8
  81.4 0.1 select_reduce_fusion.1
  81.5 0.1 convert_element_type.68
  81.6 1.0 pad_maximum_fusion
  82.6 6.3 %all-to-all-start = ((f32[8,2,40]{2,1,0:T(2,128)}), f32[8,2,40]{2,1,0:T(2,128)S(1)}, u32[]{:S(2)}, u32[]{:S(2)}) async-start(f32[8,2,40]{2,1,0:T(2,128)} %pad_maximum_fusion), calls=%async_computation | async-start | bytes 16384 | tf_op jit(solution)/shard_map/all_to_all | solution.py:176
  88.9 3.4 %copy.13 = f32[144,4608]{0,1:T(8,128)} copy(f32[144,4608]{1,0:T(8,128)S(1)} %get-tuple-element.5) | data formatting | bytes 5308416 | tf_op jit(solution)/shard_map/sub | solution.py:193
  92.3 0.0 copy-done.5
  92.3 0.1 fusion.43
  92.3 0.1 compare_reduce_fusion
  92.5 14.2 %gather_fusion = f32[4608,144]{1,0:T(8,128)} fusion(f32[144,4608]{0,1:T(8,128)} %copy.13, s32[5120]{0:T(1024)S(1)} %pad_clamp_fusion), kind=kCustom, calls=%fused_computation | custom fusion | bytes 5326848 | tf_op jit(solution)/shard_map/jit(_take)/gather | solution.py:194
  106.6 0.0 copy-done.1
  106.6 0.0 copy-start
  106.6 5.9 %fusion.15 = f32[320,4608]{1,0:T(8,128)S(1)} fusion(f32[4608,144]{1,0:T(8,128)} %gather_fusion, pred[4608]{0:T(1024)(128)(4,1)S(1)} %compare_reduce_fusion, pred[4608]{0:T(1024)(128)(4,1)S(1)} %compare_and_fusion, bf16[144]{0:T(256)(128)(2,1)S(1)} %get-tuple-element.7, s32[144]{0:T(256)S(1)} %add_select_fusion), kind=kOutput, calls=%fused_computation.24 | convolution fusion | flops 427419648 | bytes 8562528 | tf_op jit(solution)/shard_map/dot_general | solution.py:142
  112.5 0.0 copy-done
  112.5 5.4 %fusion = f16[320,4608]{1,0:T(8,128)(2,1)} fusion(f32[320,4608]{1,0:T(8,128)S(1)} %fusion.15, f32[4608,144]{1,0:T(8,128)S(1)} %copy-done, pred[4608]{0:T(1024)(128)(4,1)S(1)} %compare_reduce_fusion, pred[4608]{0:T(1024)(128)(4,1)S(1)} %compare_and_fusion, bf16[144]{0:T(256)(128)(2,1)S(1)} %get-tuple-element.7, s32[144]{0:T(256)S(1)} %add_select_fusion), kind=kOutput, calls=%fused_computation.6 | convolution fusion | flops 431695872 | bytes 11511648 | tf_op jit(solution)/shard_map/dot_general | solution.py:142
  117.9 0.0 copy-start.6
  117.9 0.0 all-to-all-done
  117.9 4.9 %all-to-all-start.1 = ((f16[8,40,4608]{2,1,0:T(8,128)(2,1)}), f16[8,40,4608]{2,1,0:T(8,128)(2,1)S(1)}, u32[]{:S(2)}, u32[]{:S(2)}) async-start(f16[8,40,4608]{2,1,0:T(8,128)(2,1)} %bitcast.41), calls=%async_computation.1 | async-start | bytes 5898240 | tf_op jit(solution)/shard_map/all_to_all | solution.py:198
  122.8 0.0 copy-done.6
  122.8 0.1 fusion.44
  122.9 2.6 %multiply_reduce_fusion = f32[144]{0:T(256)} fusion(f32[144,4608]{1,0:T(8,128)} %copy-done.1, f32[4608]{0:T(1024)S(1)} %fusion.44), kind=kLoop, calls=%fused_computation.23 | loop fusion | flops 1326960 | bytes 2673216 | tf_op jit(solution)/shard_map/reduce_sum | solution.py:201
  125.5 0.1 convert_element_type.70
  125.6 0.1 broadcast_in_dim.115
  125.7 32.6 %all-to-all-done.1 = f16[8,40,4608]{2,1,0:T(8,128)(2,1)S(1)} async-done(((f16[8,40,4608]{2,1,0:T(8,128)(2,1)}), f16[8,40,4608]{2,1,0:T(8,128)(2,1)S(1)}, u32[]{:S(2)}, u32[]{:S(2)}) %all-to-all-start.1) | async-done | bytes 2949152 | tf_op jit(solution)/shard_map/all_to_all | solution.py:198
  158.3 0.8 fusion.11
  159.2 2.5 %fusion.1 = f32[1,144,4608]{2,1,0:T(8,128)} fusion(f32[144,4608]{1,0:T(8,128)S(1)} %fusion.11, f16[320,4608]{1,0:T(8,128)(2,1)S(1)} %bitcast.40, bf16[320]{0:T(512)(128)(2,1)S(1)} %broadcast_in_dim.115, s32[320]{0:T(512)S(1)} %convert_element_type.70), kind=kOutput, calls=%fused_computation.8 | convolution fusion | flops 432801792 | bytes 8259456 | tf_op jit(solution)/shard_map/dot_general | solution.py:142
  (9 shorter events, 0.1 us)
Async XLA Ops:
  1.3 6.0 %copy-start.2 = (f32[1,1024,1024]{2,1,0:T(8,128)S(1)}, f32[1,1024,1024]{2,1,0:T(8,128)}, u32[]{:S(2)}) copy-start(f32[1,1024,1024]{2,1,0:T(8,128)} %param.10) | copy-start | bytes 12582916
  7.3 67.5 %copy-start.4 = (f32[144,1024]{1,0:T(8,128)}, f32[144,1024]{1,0:T(8,128)S(1)}, u32[]{:S(2)}) copy-start(f32[144,1024]{1,0:T(8,128)S(1)} %fusion.8) | copy-start | bytes 1769476
  10.0 64.8 %copy-start.7 = (s32[1,144,1]{1,2,0:T(1,128)S(1)}, s32[1,144,1]{1,2,0:T(1,128)}, u32[]{:S(2)}) copy-start(s32[1,144,1]{1,2,0:T(1,128)} %param.14) | copy-start | bytes 1732
  74.8 5.7 %copy-start.3 = (f32[1,144,4608]{2,1,0:T(8,128)S(1)}, f32[1,144,4608]{2,1,0:T(8,128)}, u32[]{:S(2)}) copy-start(f32[1,144,4608]{2,1,0:T(8,128)} %param.9) | copy-start | bytes 7962628
  80.5 0.9 copy-start.8
  81.1 25.5 %copy-start.1 = (f32[144,4608]{1,0:T(8,128)}, f32[144,4608]{1,0:T(8,128)S(1)}, u32[]{:S(2)}) copy-start(f32[144,4608]{1,0:T(8,128)S(1)} %get-tuple-element.5) | copy-start | bytes 7962628
  81.2 11.1 %copy-start.5 = (s32[1,4608]{1,0:T(1,128)S(1)}, s32[1,4608]{1,0:T(1,128)}, u32[]{:S(2)}) copy-start(s32[1,4608]{1,0:T(1,128)} %param.13) | copy-start | bytes 55300
  82.6 35.3 %all-to-all-start = ((f32[8,2,40]{2,1,0:T(2,128)}), f32[8,2,40]{2,1,0:T(2,128)S(1)}, u32[]{:S(2)}, u32[]{:S(2)}) async-start(f32[8,2,40]{2,1,0:T(2,128)} %pad_maximum_fusion), calls=%async_computation | async-start | bytes 16384 | tf_op jit(solution)/shard_map/all_to_all | solution.py:176
  106.6 5.9 %copy-start = (f32[4608,144]{1,0:T(8,128)S(1)}, f32[4608,144]{1,0:T(8,128)}, u32[]{:S(2)}) copy-start(f32[4608,144]{1,0:T(8,128)} %gather_fusion) | copy-start | bytes 7962628
  117.9 4.9 %copy-start.6 = (f32[1,4608]{1,0:T(1,128)S(1)}, f32[1,4608]{1,0:T(1,128)}, u32[]{:S(2)}) copy-start(f32[1,4608]{1,0:T(1,128)} %param.11) | copy-start | bytes 55300
  117.9 40.4 %all-to-all-start.1 = ((f16[8,40,4608]{2,1,0:T(8,128)(2,1)}), f16[8,40,4608]{2,1,0:T(8,128)(2,1)S(1)}, u32[]{:S(2)}, u32[]{:S(2)}) async-start(f16[8,40,4608]{2,1,0:T(8,128)(2,1)} %bitcast.41), calls=%async_computation.1 | async-start | bytes 5898240 | tf_op jit(solution)/shard_map/all_to_all | solution.py:198

commit v4 on v3

--- a/solution.py
+++ b/solution.py
@@ -10,6 +10,8 @@
 
 HIGHEST = lax.Precision.HIGHEST
 PANEL_TOP = 0.1796875
+LANES = 128
+CHUNKS = 2
 
 
 def bf16_terms(x):
@@ -148,7 +150,8 @@
     row_count = trailing.shape[1]
     col_count = trailing.shape[2]
     fronts = lax.axis_size("front")
-    capacity = -(-(row_count // 4) // 8) * 8
+    used = row_count // 4
+    capacity = -(-(used + 2) // 8) * 8
     slots = fronts * capacity
     trail_rows = trailing[0]
     inverse_rows = inverse[0]
@@ -170,16 +173,13 @@
     slot_index = jnp.sum(earlier.astype(jnp.int32), axis=1)
     flat_slot = jnp.where(live_rows, dest_front * capacity + slot_index, -1)
     place = flat_slot[None, :] == jnp.arange(slots, dtype=jnp.int32)[:, None]
-    row_tags = jnp.sum(jnp.where(place, row_offset[0][None, :] + 1, 0), axis=1) - 1
-    row_tags = row_tags.astype(jnp.float32).reshape(fronts, 1, capacity)
-    row_scales = jnp.sum(jnp.where(place, scale[None, :], 0.0), axis=1).reshape(fronts, 1, capacity)
-    received_tags = lax.all_to_all(
-        jnp.concatenate([row_tags, row_scales], axis=1),
-        "front", split_axis=0, concat_axis=0, tiled=True,
-    )
-    targets = received_tags[:, 0].reshape(slots).astype(jnp.int32)
-    scales = received_tags[:, 1].reshape(slots)
-    land = jnp.where(targets[None, :] == rows[:, None], scales[None, :], 0.0).astype(jnp.bfloat16)
+    slot_tags = jnp.sum(jnp.where(place, row_offset[0][None, :] + 1, 0), axis=1) - 1
+    exponents = jnp.round(jnp.log2(scale))
+    slot_exponents = jnp.sum(jnp.where(place, exponents[None, :], 0.0), axis=1)
+    tags = jnp.zeros((fronts, capacity, LANES), jnp.float32)
+    tags = tags.at[:, used, :capacity].set(slot_tags.astype(jnp.float32).reshape(fronts, capacity))
+    tags = tags.at[:, used + 1, :capacity].set(slot_exponents.reshape(fronts, capacity))
+    tags = tags.reshape(slots, LANES)
     spread = jnp.where(place, inverse_scale[None, :], 0.0).astype(jnp.bfloat16)
 
     columns = jnp.arange(col_count, dtype=jnp.int32)
@@ -191,17 +191,34 @@
         terms, panel_all, (((1,), (1,)), ((), ())), preferred_element_type=jnp.float32
     )
     schur = trail_rows - (update[:row_count] + update[row_count:])
-    permuted = jnp.where(keep[None, :], jnp.take(schur, source, axis=1), 0.0)
-    high, middle, _ = bf16_terms(permuted)
-    bucket = (dot_bf16(spread, high) + dot_bf16(spread, middle)).astype(jnp.float16)
-    bucket, schur = lax.optimization_barrier((bucket, schur))
-    received = lax.all_to_all(
-        bucket.reshape(fronts, capacity, col_count), "front", split_axis=0, concat_axis=0, tiled=True
-    )
+    width = col_count // CHUNKS
+    received = []
+    for chunk in range(CHUNKS):
+        part = slice(chunk * width, (chunk + 1) * width)
+        permuted = jnp.where(keep[None, part], jnp.take(schur, source[part], axis=1), 0.0)
+        high, middle, _ = bf16_terms(permuted)
+        bucket = dot_bf16(spread, high) + dot_bf16(spread, middle)
+        if chunk == 0:
+            bucket = bucket + jnp.pad(tags, ((0, 0), (0, width - LANES)))
+        bucket = bucket.astype(jnp.float16)
+        bucket, source, masked_weights = lax.optimization_barrier((bucket, source, masked_weights))
+        received.append(
+            lax.all_to_all(
+                bucket.reshape(fronts, capacity, width),
+                "front", split_axis=0, concat_axis=0, tiled=True,
+            )
+        )
     checksum = jnp.sum(schur * masked_weights[None, :], axis=1)
-    received = received.reshape(slots, col_count).astype(jnp.float32)
-    high, middle, _ = bf16_terms(received)
-    ancestor = dot_bf16(land, high) + dot_bf16(land, middle)
+
+    heads = received[0][:, used : used + 2, :capacity].astype(jnp.float32)
+    targets = heads[:, 0].reshape(slots).astype(jnp.int32)
+    scales = lax.reduce_precision(jnp.exp2(heads[:, 1].reshape(slots)), 8, 0)
+    land = jnp.where(targets[None, :] == rows[:, None], scales[None, :], 0.0).astype(jnp.bfloat16)
+    ancestor = []
+    for block in received:
+        high, middle, _ = bf16_terms(block.reshape(slots, width).astype(jnp.float32))
+        ancestor.append(dot_bf16(land, high) + dot_bf16(land, middle))
+    ancestor = jnp.concatenate(ancestor, axis=1)
     return (factor[None], checksum[None], ancestor[None])
 
 

time: 162 us -> 157 us (0.969)
  waiting for transfers between devices: 32.6 us -> 18.4 us
  matrix products: 27.9 us -> 34.2 us
  local copies, waits for them, and re-layouts: 17.9 us -> 21.7 us
    all_to_all x2, waiting for transfers between devices: 32.6 us -> 18.4 us  [on_device(): lax.all_to_all(bucket.reshape(fronts, capacity, width), 'front', split_ax...]
    dot_general x4 -> x8, matrix products: 14.6 us -> 21 us  [dot_bf16(): return jnp.dot(a, b, preferred_element_type=jnp.float32)]
    gather x1 -> x2, local copies, waits for them, and re-layouts: 14.2 us -> 17.6 us  [on_device(): jnp.take(schur, source[part], axis=1)]
    broadcast_in_dim x0 -> x1, other arithmetic: none -> 1.79 us  [on_device(): return (factor[None], checksum[None], ancestor[None])]
    reduce_sum x1, other arithmetic: 2.62 us -> 0.86 us  [on_device(): checksum = jnp.sum(schur * masked_weights[None, :], axis=1)]
  transfers between devices with their start and end apart: 2 -> 2, of which waited for: 1 -> 2; matrix products, arithmetic and copies ran while one was open for 20% -> 13% of each run, Pallas kernels for 0% -> 0%
where the time goes in v4:
time: 157 us
  Pallas kernels  64.8 us (41%)
  matrix products  34.2 us (22%)
  local copies, waits for them, and re-layouts  21.7 us (14%)
  waiting for transfers between devices  18.4 us (12%)
  starting transfers between devices  11.4 us (7%)
  other arithmetic  4.68 us (3%)
  between operations  1.61 us (1%)
    pallas_call x1, Pallas kernels, gather_panels(): pl.pallas_call(functools.partial(gather_kernel, plan), out_shape=jax.Shap...  64.8 us
    dot_general x8, matrix products, dot_bf16(): return jnp.dot(a, b, preferred_element_type=jnp.float32)  21 us
    all_to_all x2, waiting for transfers between devices, on_device(): lax.all_to_all(bucket.reshape(fronts, capacity, width), 'front', split_ax...  18.4 us
    gather x2, local copies, waits for them, and re-layouts, on_device(): jnp.take(schur, source[part], axis=1)  17.6 us
    all_to_all x2, starting transfers between devices, on_device(): lax.all_to_all(bucket.reshape(fronts, capacity, width), 'front', split_ax...  11.4 us
    dot_general x1, matrix products, on_device(): lax.dot_general(terms, panel_all, (((1,), (1,)), ((), ())), preferred_ele...  5.68 us
    dot_general x1, matrix products, on_device(): factor = jnp.dot(panel_f32, inverse_rows.T, precision=HIGHEST)  4.86 us
    sub x1, local copies, waits for them, and re-layouts, on_device(): schur = trail_rows - (update[:row_count] + update[row_count:])  3.37 us
  transfers between devices with their start and end apart: 2, of which 2 were waited for; matrix products, arithmetic and copies ran while one was open for 13% of the time, Pallas kernels for 0%

profile of v4, /device:TPU:1, one launch (start us, length us, event | category | flops | bytes accessed | tf_op | source)
XLA Modules:
  0.0 156.8 jit_solution(2791920601793955491)
XLA Ops:
  0.6 0.0 copy-start
  0.6 4.9 %fusion.3 = f32[144,1024]{1,0:T(8,128)S(1)} fusion(f32[1,1024,1024]{2,1,0:T(8,128)} %param.16, bf16[1,144,1024]{2,1,0:T(8,128)(2,1)} %param.14), kind=kOutput, calls=%fused_computation.11 | convolution fusion | flops 1811939328 | bytes 5079040 | tf_op jit(solution)/shard_map/dot_general | solution.py:162
  5.5 0.0 copy-done
  5.5 0.0 copy-start.4
  5.5 2.7 %abs_reduce_fusion = (f32[144]{0:T(256)S(1)}, bf16[144,1024]{1,0:T(8,128)(2,1)S(1)}, bf16[144,1024]{1,0:T(8,128)(2,1)S(1)}) fusion(f32[144,1024]{1,0:T(8,128)S(1)} %fusion.3, f32[1,1024,1024]{2,1,0:T(8,128)S(1)} %copy-done), kind=kOutput, calls=%fused_computation.65 | convolution fusion | flops 1812971392 | bytes 5374528 | tf_op jit(solution)/shard_map/dot_general | solution.py:163
  8.2 0.0 copy-done.4
  8.2 64.8 %shard_map.103 = bf16[4,8,144,1024]{3,2,1,0:T(8,128)(2,1)} custom-call(bf16[144,1024]{1,0:T(8,128)(2,1)} %bitcast.56), custom_call_target="tpu_custom_call" | custom-call | tf_op jit(solution)/shard_map/pallas_call | solution.py:128
  73.0 0.0 copy-start.3
  73.0 5.7 %fusion.43 = f32[288,4608]{1,0:T(8,128)S(1)} fusion(bf16[4608,1024]{1,0:T(8,128)(2,1)} %bitcast.52, bf16[144,1024]{1,0:T(8,128)(2,1)S(1)} %get-tuple-element.41, bf16[144,1024]{1,0:T(8,128)(2,1)S(1)} %get-tuple-element.42), kind=kOutput, calls=%fused_computation.61 | convolution fusion | flops 2719088640 | bytes 15335424 | tf_op jit(solution)/shard_map/dot_general | solution.py:190
  78.7 0.0 copy-done.3
  78.7 0.0 copy-start.7
  78.7 0.6 fusion.12
  80.0 0.0 copy-done.7
  80.1 0.2 convert_reduce_fusion
  80.3 0.0 copy-start.5
  80.3 0.0 copy-start.8
  80.3 3.4 %copy.13 = f32[144,4608]{0,1:T(8,128)} copy(f32[144,4608]{1,0:T(8,128)S(1)} %get-tuple-element.39) | data formatting | bytes 5308416 | tf_op jit(solution)/shard_map/sub | solution.py:193
  83.7 0.0 copy-done.5
  83.8 0.1 select_reduce_fusion
  83.9 0.1 reshape.192
  84.0 0.0 copy-done.8
  84.0 0.1 select_reduce_fusion.1
  84.2 0.1 convert_element_type.94
  84.3 8.8 %gather_fusion = f32[2304,144]{1,0:T(8,128)} fusion(f32[144,4608]{0,1:T(8,128)} %copy.13, s32[3072]{0:T(1024)S(1)} %pad_clamp_fusion.1), kind=kCustom, calls=%fused_computation.clone | custom fusion | bytes 2663424 | tf_op jit(solution)/shard_map/jit(_take)/gather | solution.py:198
  93.1 0.3 scatter.9
  93.4 0.0 copy-start.2
  93.4 3.5 %fusion.23 = f32[320,2304]{1,0:T(8,128)S(1)} fusion(f32[2304,144]{1,0:T(8,128)} %gather_fusion, pred[2304]{0:T(1024)(128)(4,1)S(1)} %get-tuple-element.45, pred[2304]{0:T(1024)(128)(4,1)S(1)} %get-tuple-element.44, bf16[144]{0:T(256)(128)(2,1)S(1)} %divide_reduce-precision_fusion, s32[144]{0:T(256)S(1)} %add_select_fusion), kind=kOutput, calls=%fused_computation.39 | convolution fusion | flops 213755904 | bytes 4281696 | tf_op jit(solution)/shard_map/dot_general | solution.py:144
  96.9 0.0 copy-done.2
  96.9 0.0 copy-start.6
  96.9 3.2 %fusion.5 = f16[320,2304]{1,0:T(8,128)(2,1)} fusion(f32[320,2304]{1,0:T(8,128)S(1)} %fusion.23, f32[320,128]{1,0:T(8,128)S(1)} %bitcast.57, f32[2304,144]{1,0:T(8,128)S(1)} %copy-done.2, pred[2304]{0:T(1024)(128)(4,1)S(1)} %get-tuple-element.45, pred[2304]{0:T(1024)(128)(4,1)S(1)} %get-tuple-element.44, bf16[144]{0:T(256)(128)(2,1)S(1)} %divide_reduce-precision_fusion, ...), kind=kOutput, calls=%fused_computation.13 | convolution fusion | flops 216631296 | bytes 5920096 | tf_op jit(solution)/shard_map/dot_general | solution.py:144
  100.1 0.0 copy-done.6
  100.2 6.4 %all-to-all-start = ((f16[8,40,2304]{2,1,0:T(8,128)(2,1)}), f16[8,40,2304]{2,1,0:T(8,128)(2,1)}, u32[]{:S(2)}, u32[]{:S(2)}) async-start(f16[8,40,2304]{2,1,0:T(8,128)(2,1)} %bitcast.55), calls=%async_computation | async-start | bytes 2949120 | tf_op jit(solution)/shard_map/all_to_all | solution.py:206
  106.6 8.8 %gather_fusion.1 = f32[2304,144]{1,0:T(8,128)} fusion(f32[144,4608]{0,1:T(8,128)} %copy.13, s32[3072]{0:T(1024)S(1)} %pad_clamp_fusion), kind=kCustom, calls=%fused_computation.1.clone | custom fusion | bytes 2663424 | tf_op jit(solution)/shard_map/jit(_take)/gather | solution.py:198
  115.4 0.0 copy-start.1
  115.4 3.5 %fusion.24 = f32[320,2304]{1,0:T(8,128)S(1)} fusion(f32[2304,144]{1,0:T(8,128)} %gather_fusion.1, pred[2304]{0:T(1024)(128)(4,1)S(1)} %compare_and_fusion, pred[2304]{0:T(1024)(128)(4,1)S(1)} %get-tuple-element.43, bf16[144]{0:T(256)(128)(2,1)S(1)} %divide_reduce-precision_fusion, s32[144]{0:T(256)S(1)} %add_select_fusion), kind=kOutput, calls=%fused_computation.40 | convolution fusion | flops 213755904 | bytes 4281696 | tf_op jit(solution)/shard_map/dot_general | solution.py:144
  118.9 3.2 %fusion.6 = f16[320,2304]{1,0:T(8,128)(2,1)} fusion(f32[320,2304]{1,0:T(8,128)S(1)} %fusion.24, f32[2304,144]{1,0:T(8,128)S(1)} %copy-done.1, pred[2304]{0:T(1024)(128)(4,1)S(1)} %compare_and_fusion, pred[2304]{0:T(1024)(128)(4,1)S(1)} %get-tuple-element.43, bf16[144]{0:T(256)(128)(2,1)S(1)} %divide_reduce-precision_fusion, s32[144]{0:T(256)S(1)} %add_select_fusion), kind=kOutput, calls=%fused_computation.14 | convolution fusion | flops 215894016 | bytes 5756256 | tf_op jit(solution)/shard_map/dot_general | solution.py:144
  122.1 4.3 %all-to-all-done = f16[8,40,2304]{2,1,0:T(8,128)(2,1)} async-done(((f16[8,40,2304]{2,1,0:T(8,128)(2,1)}), f16[8,40,2304]{2,1,0:T(8,128)(2,1)}, u32[]{:S(2)}, u32[]{:S(2)}) %all-to-all-start) | async-done | bytes 1474592 | tf_op jit(solution)/shard_map/all_to_all | solution.py:206
  126.3 5.0 %all-to-all-start.1 = ((f16[8,40,2304]{2,1,0:T(8,128)(2,1)}), f16[8,40,2304]{2,1,0:T(8,128)(2,1)}, u32[]{:S(2)}, u32[]{:S(2)}) async-start(f16[8,40,2304]{2,1,0:T(8,128)(2,1)} %bitcast.53), calls=%async_computation.1 | async-start | bytes 2949120 | tf_op jit(solution)/shard_map/all_to_all | solution.py:206
  131.4 0.9 multiply_reduce_fusion
  132.2 0.7 slice_convert_fusion.1
  133.0 0.1 convert_element_type.101
  133.1 0.1 reduce_precision.66
  133.2 1.9 %fusion.19 = f32[144,2304]{1,0:T(8,128)S(1)} fusion(f16[320,2304]{1,0:T(8,128)(2,1)} %bitcast.14, bf16[320]{0:T(512)(128)(2,1)S(1)} %reduce_precision.66, s32[320]{0:T(512)S(1)} %convert_element_type.101), kind=kOutput, calls=%fused_computation.37 | convolution fusion | flops 214640640 | bytes 2803584 | tf_op jit(solution)/shard_map/dot_general | solution.py:144
  135.1 1.9 %convolution_add_fusion.3 = f32[144,2304]{1,0:T(8,128)S(1)} fusion(f32[144,2304]{1,0:T(8,128)S(1)} %fusion.19, f16[320,2304]{1,0:T(8,128)(2,1)} %bitcast.14, bf16[320]{0:T(512)(128)(2,1)S(1)} %reduce_precision.66, s32[320]{0:T(512)S(1)} %convert_element_type.101), kind=kOutput, calls=%fused_computation.16 | convolution fusion | flops 216446976 | bytes 4130688 | tf_op jit(solution)/shard_map/dot_general | solution.py:144
  137.0 14.1 %all-to-all-done.1 = f16[8,40,2304]{2,1,0:T(8,128)(2,1)} async-done(((f16[8,40,2304]{2,1,0:T(8,128)(2,1)}), f16[8,40,2304]{2,1,0:T(8,128)(2,1)}, u32[]{:S(2)}, u32[]{:S(2)}) %all-to-all-start.1) | async-done | bytes 1474592 | tf_op jit(solution)/shard_map/all_to_all | solution.py:206
  151.2 1.9 %fusion.20 = f32[144,2304]{1,0:T(8,128)S(1)} fusion(f16[320,2304]{1,0:T(8,128)(2,1)} %bitcast.17, bf16[320]{0:T(512)(128)(2,1)S(1)} %reduce_precision.66, s32[320]{0:T(512)S(1)} %convert_element_type.101), kind=kOutput, calls=%fused_computation.38 | convolution fusion | flops 214640640 | bytes 2803584 | tf_op jit(solution)/shard_map/dot_general | solution.py:144
  153.1 1.9 %convolution_add_fusion.2 = f32[144,2304]{1,0:T(8,128)S(1)} fusion(f32[144,2304]{1,0:T(8,128)S(1)} %fusion.20, f16[320,2304]{1,0:T(8,128)(2,1)} %bitcast.17, bf16[320]{0:T(512)(128)(2,1)S(1)} %reduce_precision.66, s32[320]{0:T(512)S(1)} %convert_element_type.101), kind=kOutput, calls=%fused_computation.15 | convolution fusion | flops 216446976 | bytes 4130688 | tf_op jit(solution)/shard_map/dot_general | solution.py:144
  155.0 1.8 %maximum_bitcast_fusion = f32[1,144,4608]{2,1,0:T(8,128)} fusion(f32[144,2304]{1,0:T(8,128)S(1)} %convolution_add_fusion.2, f32[144,2304]{1,0:T(8,128)S(1)} %convolution_add_fusion.3), kind=kLoop, calls=%fused_computation.27 | loop fusion | flops 663552 | bytes 5308416 | tf_op jit(solution)/shard_map/broadcast_in_dim | solution.py:222
  (21 shorter events, 0.3 us)
Async XLA Ops:
  0.6 4.9 %copy-start = (f32[1,1024,1024]{2,1,0:T(8,128)S(1)}, f32[1,1024,1024]{2,1,0:T(8,128)}, u32[]{:S(2)}) copy-start(f32[1,1024,1024]{2,1,0:T(8,128)} %param.16) | copy-start | bytes 12582916
  5.5 2.7 %copy-start.4 = (f32[144,1024]{1,0:T(8,128)}, f32[144,1024]{1,0:T(8,128)S(1)}, u32[]{:S(2)}) copy-start(f32[144,1024]{1,0:T(8,128)S(1)} %fusion.3) | copy-start | bytes 1769476
  73.0 5.7 %copy-start.3 = (f32[1,144,4608]{2,1,0:T(8,128)S(1)}, f32[1,144,4608]{2,1,0:T(8,128)}, u32[]{:S(2)}) copy-start(f32[1,144,4608]{2,1,0:T(8,128)} %param.15) | copy-start | bytes 7962628
  78.7 1.3 copy-start.7
  80.3 3.4 %copy-start.5 = (s32[1,4608]{1,0:T(1,128)S(1)}, s32[1,4608]{1,0:T(1,128)}, u32[]{:S(2)}) copy-start(s32[1,4608]{1,0:T(1,128)} %param.19) | copy-start | bytes 55300
  80.3 3.8 %copy-start.8 = (s32[1,144]{1,0:T(1,128)S(1)}, s32[1,144]{1,0:T(1,128)}, u32[]{:S(2)}) copy-start(s32[1,144]{1,0:T(1,128)} %param.21) | copy-start | bytes 1732
  93.4 3.5 %copy-start.2 = (f32[2304,144]{1,0:T(8,128)S(1)}, f32[2304,144]{1,0:T(8,128)}, u32[]{:S(2)}) copy-start(f32[2304,144]{1,0:T(8,128)} %gather_fusion) | copy-start | bytes 3981316
  96.9 3.3 %copy-start.6 = (f32[1,4608]{1,0:T(1,128)S(1)}, f32[1,4608]{1,0:T(1,128)}, u32[]{:S(2)}) copy-start(f32[1,4608]{1,0:T(1,128)} %param.17) | copy-start | bytes 55300
  100.2 26.2 %all-to-all-start = ((f16[8,40,2304]{2,1,0:T(8,128)(2,1)}), f16[8,40,2304]{2,1,0:T(8,128)(2,1)}, u32[]{:S(2)}, u32[]{:S(2)}) async-start(f16[8,40,2304]{2,1,0:T(8,128)(2,1)} %bitcast.55), calls=%async_computation | async-start | bytes 2949120 | tf_op jit(solution)/shard_map/all_to_all | solution.py:206
  115.4 3.5 %copy-start.1 = (f32[2304,144]{1,0:T(8,128)S(1)}, f32[2304,144]{1,0:T(8,128)}, u32[]{:S(2)}) copy-start(f32[2304,144]{1,0:T(8,128)} %gather_fusion.1) | copy-start | bytes 3981316
  126.3 24.8 %all-to-all-start.1 = ((f16[8,40,2304]{2,1,0:T(8,128)(2,1)}), f16[8,40,2304]{2,1,0:T(8,128)(2,1)}, u32[]{:S(2)}, u32[]{:S(2)}) async-start(f16[8,40,2304]{2,1,0:T(8,128)(2,1)} %bitcast.53), calls=%async_computation.1 | async-start | bytes 2949120 | tf_op jit(solution)/shard_map/all_to_all | solution.py:206

commit v5 on v4

--- a/solution.py
+++ b/solution.py
@@ -11,7 +11,6 @@
 HIGHEST = lax.Precision.HIGHEST
 PANEL_TOP = 0.1796875
 LANES = 128
-CHUNKS = 2
 
 
 def bf16_terms(x):
@@ -140,10 +139,6 @@
     return gathered.reshape(RINGS[0] * RINGS[1] * rows, width)
 
 
-def dot_bf16(a, b):
-    return jnp.dot(a, b, preferred_element_type=jnp.float32)
-
-
 def on_device(
     panel_block, trailing, inverse, weights, live_size, column_source, destination, row_offset
 ):
@@ -180,7 +175,7 @@
     tags = tags.at[:, used, :capacity].set(slot_tags.astype(jnp.float32).reshape(fronts, capacity))
     tags = tags.at[:, used + 1, :capacity].set(slot_exponents.reshape(fronts, capacity))
     tags = tags.reshape(slots, LANES)
-    spread = jnp.where(place, inverse_scale[None, :], 0.0).astype(jnp.bfloat16)
+    spread = jnp.where(place, inverse_scale[None, :], 0.0)
 
     columns = jnp.arange(col_count, dtype=jnp.int32)
     keep = source < live_count
@@ -191,14 +186,14 @@
         terms, panel_all, (((1,), (1,)), ((), ())), preferred_element_type=jnp.float32
     )
     schur = trail_rows - (update[:row_count] + update[row_count:])
-    width = col_count // CHUNKS
+    early = col_count * 2 // 5 // LANES * LANES
     received = []
-    for chunk in range(CHUNKS):
-        part = slice(chunk * width, (chunk + 1) * width)
+    for begin, end in ((0, early), (early, col_count)):
+        part = slice(begin, end)
+        width = end - begin
         permuted = jnp.where(keep[None, part], jnp.take(schur, source[part], axis=1), 0.0)
-        high, middle, _ = bf16_terms(permuted)
-        bucket = dot_bf16(spread, high) + dot_bf16(spread, middle)
-        if chunk == 0:
+        bucket = jnp.dot(spread, permuted, precision=lax.Precision.HIGH)
+        if begin == 0:
             bucket = bucket + jnp.pad(tags, ((0, 0), (0, width - LANES)))
         bucket = bucket.astype(jnp.float16)
         bucket, source, masked_weights = lax.optimization_barrier((bucket, source, masked_weights))
@@ -213,11 +208,11 @@
     heads = received[0][:, used : used + 2, :capacity].astype(jnp.float32)
     targets = heads[:, 0].reshape(slots).astype(jnp.int32)
     scales = lax.reduce_precision(jnp.exp2(heads[:, 1].reshape(slots)), 8, 0)
-    land = jnp.where(targets[None, :] == rows[:, None], scales[None, :], 0.0).astype(jnp.bfloat16)
+    land = jnp.where(targets[None, :] == rows[:, None], scales[None, :], 0.0)
     ancestor = []
     for block in received:
-        high, middle, _ = bf16_terms(block.reshape(slots, width).astype(jnp.float32))
-        ancestor.append(dot_bf16(land, high) + dot_bf16(land, middle))
+        block = block.reshape(slots, -1).astype(jnp.float32)
+        ancestor.append(jnp.dot(land, block, precision=lax.Precision.HIGH))
     ancestor = jnp.concatenate(ancestor, axis=1)
     return (factor[None], checksum[None], ancestor[None])
 

time: 157 us -> 159 us (1.013)
    dot_general x8 -> x4, matrix products: 21 us -> 18.7 us  [the longest x2 13.1 us: on_device(): bucket = jnp.dot(spread, permuted, precision=lax.Precision.HIGH)]
    dot_general x1, matrix products: 2.7 us -> 4.87 us  [on_device(): twice = jnp.dot(factor, inverse_rows, precision=HIGHEST)]
  transfers between devices with their start and end apart: 2 -> 2, of which waited for: 2 -> 1; matrix products, arithmetic and copies ran while one was open for 13% -> 14% of each run, Pallas kernels for 0% -> 0%
where the time goes in v5:
time: 159 us; the launch traced here: 158 us
  Pallas kernels  64.8 us (41%)
  matrix products  34.1 us (21%)
  local copies, waits for them, and re-layouts  22.4 us (14%)
  waiting for transfers between devices  19.1 us (12%)
  starting transfers between devices  11.1 us (7%)
  other arithmetic  5.38 us (3%)
    pallas_call x1, Pallas kernels, gather_panels(): pl.pallas_call(functools.partial(gather_kernel, plan), out_shape=jax.Shap...  64.8 us
    all_to_all x2, waiting for transfers between devices, on_device(): lax.all_to_all(bucket.reshape(fronts, capacity, width), 'front', split_ax...  19.1 us
    gather x2, local copies, waits for them, and re-layouts, on_device(): jnp.take(schur, source[part], axis=1)  17.6 us
    dot_general x2, matrix products, on_device(): bucket = jnp.dot(spread, permuted, precision=lax.Precision.HIGH)  13.1 us
    all_to_all x2, starting transfers between devices, on_device(): lax.all_to_all(bucket.reshape(fronts, capacity, width), 'front', split_ax...  11.1 us
    dot_general x1, matrix products, on_device(): lax.dot_general(terms, panel_all, (((1,), (1,)), ((), ())), preferred_ele...  5.86 us
    dot_general x2, matrix products, on_device(): ancestor.append(jnp.dot(land, block, precision=lax.Precision.HIGH))  5.55 us
    dot_general x1, matrix products, on_device(): twice = jnp.dot(factor, inverse_rows, precision=HIGHEST)  4.87 us
  transfers between devices with their start and end apart: 2, of which 1 were waited for; matrix products, arithmetic and copies ran while one was open for 14% of the time, Pallas kernels for 0%

profile of v5, /device:TPU:1, one launch (start us, length us, event | category | flops | bytes accessed | tf_op | source)
XLA Modules:
  0.0 158.5 jit_solution(6403202509603522348)
XLA Ops:
  0.6 0.7 fusion.45
  1.4 0.7 slice_reduce_fusion
  2.1 4.7 %fusion.2 = f32[144,1024]{1,0:T(8,128)S(1)} fusion(f32[1,1024,1024]{2,1,0:T(8,128)} %param.14, bf16[1,144,1024]{2,1,0:T(8,128)(2,1)} %param.12), kind=kOutput, calls=%fused_computation.4 | convolution fusion | flops 1811939328 | bytes 5079040 | tf_op jit(solution)/shard_map/dot_general | solution.py:157
  6.8 0.0 copy-start.1
  6.8 64.8 %shard_map.103 = bf16[4,8,144,1024]{3,2,1,0:T(8,128)(2,1)} custom-call(bf16[144,1024]{1,0:T(8,128)(2,1)} %bitcast.41), custom_call_target="tpu_custom_call" | custom-call | tf_op jit(solution)/shard_map/pallas_call | solution.py:127
  71.7 0.0 copy-done.1
  71.7 4.9 %abs_reduce_fusion = (f32[144]{0:T(256)S(1)}, bf16[144,1024]{1,0:T(8,128)(2,1)S(1)}, bf16[144,1024]{1,0:T(8,128)(2,1)S(1)}) fusion(f32[144,1024]{1,0:T(8,128)S(1)} %fusion.2, f32[1,1024,1024]{2,1,0:T(8,128)} %param.14), kind=kOutput, calls=%fused_computation.35 | convolution fusion | flops 1812971392 | bytes 5374528 | tf_op jit(solution)/shard_map/dot_general | solution.py:158
  76.5 0.0 copy-start
  76.5 5.9 %fusion.21 = f32[288,4608]{1,0:T(8,128)S(1)} fusion(bf16[4608,1024]{1,0:T(8,128)(2,1)} %bitcast.38, bf16[144,1024]{1,0:T(8,128)(2,1)S(1)} %get-tuple-element.40, bf16[144,1024]{1,0:T(8,128)(2,1)S(1)} %get-tuple-element.41), kind=kOutput, calls=%fused_computation.31 | convolution fusion | flops 2719088640 | bytes 15335424 | tf_op jit(solution)/shard_map/dot_general | solution.py:185
  82.4 0.0 copy-done
  82.4 0.6 fusion.8
  83.0 0.0 copy-start.5
  83.0 0.0 copy-start.4
  83.1 0.0 copy-start.2
  83.1 3.4 %copy.15 = f32[144,4608]{0,1:T(8,128)} copy(f32[144,4608]{1,0:T(8,128)S(1)} %get-tuple-element.38) | data formatting | bytes 5308416 | tf_op jit(solution)/shard_map/sub | solution.py:188
  86.4 0.0 copy-done.5
  87.1 0.0 copy-done.4
  87.1 0.2 convert_reduce_fusion
  87.3 0.1 select_reduce_fusion.1
  87.5 0.1 convert_element_type.51
  87.6 0.1 select_reduce_fusion
  87.7 0.1 reshape.226
  87.8 0.0 copy-done.2
  87.9 0.0 copy-start.3
  87.9 7.6 %gather_fusion = f32[1792,144]{1,0:T(8,128)} fusion(f32[144,4608]{0,1:T(8,128)} %copy.15, s32[2048]{0:T(1024)S(1)} %pad_clamp_fusion.1), kind=kCustom, calls=%fused_computation | custom fusion | bytes 2071552 | tf_op jit(solution)/shard_map/jit(_take)/gather | solution.py:194
  95.6 0.0 copy-done.3
  95.6 0.3 scatter.9
  95.9 5.3 %fusion.6 = f16[320,1792]{1,0:T(8,128)(2,1)} fusion(f32[320,128]{1,0:T(8,128)S(1)} %bitcast.43, f32[1792,144]{1,0:T(8,128)} %gather_fusion, pred[1792]{0:T(1024)(128)(4,1)S(1)} %slice.101, pred[1792]{0:T(1024)(128)(4,1)S(1)} %compare_and_fusion.1, f32[144]{0:T(256)S(1)} %get-tuple-element.42, s32[144]{0:T(256)S(1)} %add_select_fusion), kind=kOutput, calls=%fused_computation.10 | convolution fusion | flops 497207296 | bytes 2347648 | tf_op jit(solution)/shard_map/dot_general | solution.py:195
  101.2 6.3 %all-to-all-start = ((f16[8,40,1792]{2,1,0:T(8,128)(2,1)}), f16[8,40,1792]{2,1,0:T(8,128)(2,1)}, u32[]{:S(2)}, u32[]{:S(2)}) async-start(f16[8,40,1792]{2,1,0:T(8,128)(2,1)} %bitcast.42), calls=%async_computation | async-start | bytes 2293760 | tf_op jit(solution)/shard_map/all_to_all | solution.py:201
  107.6 10.0 %gather_fusion.1 = f32[2816,144]{1,0:T(8,128)} fusion(f32[144,4608]{0,1:T(8,128)} %copy.15, s32[3072]{0:T(1024)S(1)} %pad_clamp_fusion), kind=kCustom, calls=%fused_computation.1 | custom fusion | bytes 3255296 | tf_op jit(solution)/shard_map/jit(_take)/gather | solution.py:194
  117.6 7.8 %convolution_convert_fusion = f16[320,2816]{1,0:T(8,128)(2,1)} fusion(f32[2816,144]{1,0:T(8,128)} %gather_fusion.1, pred[2816]{0:T(1024)(128)(4,1)S(1)} %slice.100, pred[2816]{0:T(1024)(128)(4,1)S(1)} %compare_and_fusion, f32[144]{0:T(256)S(1)} %get-tuple-element.42, s32[144]{0:T(256)S(1)} %add_select_fusion), kind=kOutput, calls=%fused_computation.6 | convolution fusion | flops 780371968 | bytes 3431040 | tf_op jit(solution)/shard_map/dot_general | solution.py:195
  125.4 0.0 all-to-all-done
  125.4 4.8 %all-to-all-start.1 = ((f16[8,40,2816]{2,1,0:T(8,128)(2,1)}), f16[8,40,2816]{2,1,0:T(8,128)(2,1)}, u32[]{:S(2)}, u32[]{:S(2)}) async-start(f16[8,40,2816]{2,1,0:T(8,128)(2,1)} %bitcast.39), calls=%async_computation.1 | async-start | bytes 3604480 | tf_op jit(solution)/shard_map/all_to_all | solution.py:201
  130.2 0.9 multiply_reduce_fusion
  131.1 0.7 slice_convert_fusion.1
  131.8 0.1 reduce_precision.38
  131.9 0.1 convert_element_type.56
  132.0 2.4 %fusion.27 = f32[144,1792]{1,0:T(8,128)S(1)} fusion(f16[320,1792]{1,0:T(8,128)(2,1)} %bitcast.12, f32[320]{0:T(512)S(1)} %reduce_precision.38, s32[320]{0:T(512)S(1)} %convert_element_type.56), kind=kOutput, calls=%fused_computation.38 | convolution fusion | flops 495544320 | bytes 2181632 | tf_op jit(solution)/shard_map/dot_general | solution.py:215
  134.4 19.1 %all-to-all-done.1 = f16[8,40,2816]{2,1,0:T(8,128)(2,1)} async-done(((f16[8,40,2816]{2,1,0:T(8,128)(2,1)}), f16[8,40,2816]{2,1,0:T(8,128)(2,1)}, u32[]{:S(2)}, u32[]{:S(2)}) %all-to-all-start.1) | async-done | bytes 1802272 | tf_op jit(solution)/shard_map/all_to_all | solution.py:201
  153.5 3.2 %fusion.25 = f32[144,2816]{1,0:T(8,128)S(1)} fusion(f16[320,2816]{1,0:T(8,128)(2,1)} %bitcast.14, f32[320]{0:T(512)S(1)} %reduce_precision.38, s32[320]{0:T(512)S(1)} %convert_element_type.56), kind=kOutput, calls=%fused_computation.36 | convolution fusion | flops 778659840 | bytes 3426816 | tf_op jit(solution)/shard_map/dot_general | solution.py:215
  156.7 1.8 %maximum_bitcast_fusion = f32[1,144,4608]{2,1,0:T(8,128)} fusion(f32[144,2816]{1,0:T(8,128)S(1)} %fusion.25, f32[144,1792]{1,0:T(8,128)S(1)} %fusion.27), kind=kLoop, calls=%fused_computation.13 | loop fusion | flops 663552 | bytes 5308416 | tf_op jit(solution)/shard_map/broadcast_in_dim | solution.py:217
  (19 shorter events, 0.3 us)
Async XLA Ops:
  6.8 64.9 %copy-start.1 = (f32[144,1024]{1,0:T(8,128)}, f32[144,1024]{1,0:T(8,128)S(1)}, u32[]{:S(2)}) copy-start(f32[144,1024]{1,0:T(8,128)S(1)} %fusion.2) | copy-start | bytes 1769476
  76.5 5.9 %copy-start = (f32[1,144,4608]{2,1,0:T(8,128)S(1)}, f32[1,144,4608]{2,1,0:T(8,128)}, u32[]{:S(2)}) copy-start(f32[1,144,4608]{2,1,0:T(8,128)} %param.13) | copy-start | bytes 7962628
  83.0 3.4 %copy-start.5 = (s32[1,144]{1,0:T(1,128)S(1)}, s32[1,144]{1,0:T(1,128)}, u32[]{:S(2)}) copy-start(s32[1,144]{1,0:T(1,128)} %param.19) | copy-start | bytes 1732
  83.0 4.1 %copy-start.4 = (s32[1,144,1]{1,2,0:T(1,128)S(1)}, s32[1,144,1]{1,2,0:T(1,128)}, u32[]{:S(2)}) copy-start(s32[1,144,1]{1,2,0:T(1,128)} %param.18) | copy-start | bytes 1732
  83.1 4.8 %copy-start.2 = (s32[1,4608]{1,0:T(1,128)S(1)}, s32[1,4608]{1,0:T(1,128)}, u32[]{:S(2)}) copy-start(s32[1,4608]{1,0:T(1,128)} %param.17) | copy-start | bytes 55300
  87.9 7.6 %copy-start.3 = (f32[1,4608]{1,0:T(1,128)S(1)}, f32[1,4608]{1,0:T(1,128)}, u32[]{:S(2)}) copy-start(f32[1,4608]{1,0:T(1,128)} %param.15) | copy-start | bytes 55300
  101.2 24.2 %all-to-all-start = ((f16[8,40,1792]{2,1,0:T(8,128)(2,1)}), f16[8,40,1792]{2,1,0:T(8,128)(2,1)}, u32[]{:S(2)}, u32[]{:S(2)}) async-start(f16[8,40,1792]{2,1,0:T(8,128)(2,1)} %bitcast.42), calls=%async_computation | async-start | bytes 2293760 | tf_op jit(solution)/shard_map/all_to_all | solution.py:201
  125.4 28.1 %all-to-all-start.1 = ((f16[8,40,2816]{2,1,0:T(8,128)(2,1)}), f16[8,40,2816]{2,1,0:T(8,128)(2,1)}, u32[]{:S(2)}, u32[]{:S(2)}) async-start(f16[8,40,2816]{2,1,0:T(8,128)(2,1)} %bitcast.39), calls=%async_computation.1 | async-start | bytes 3604480 | tf_op jit(solution)/shard_map/all_to_all | solution.py:201
